TPU v7x, 256 devices: a whole 4x4x8 slice. The times are simulated.
256 devices in a mesh: frow: 16 (over z, x_lo), fcol: 16 (over y, x_hi, core).
Axes of the slice: x: 4 (x_hi: 2, x_lo: 2; x = x_hi * 2 + x_lo), y: 4, z: 8, core: 2. Of those that a mesh axis runs over, the one named last changes fastest.
Arguments:
- facets: float32 [2, 2048, 16384], P(None, 'frow', 'fcol'), may hold values from -6 to 6
- column_start: int32 [1], replicated, may hold values from 0 to 16383
- subgrid_start: int32 [16], replicated, may hold values from 0 to 2047
- vis_count: int32 [16], P('frow'), may hold values from 1 to 64
- vis_row: int32 [16, 64], P('frow'), may hold values from 0 to 511
- vis_weight: float32 [16, 64, 512], P('frow', None, 'fcol'), may hold values from -1 to 1
Outputs:
- corrected: float32 [16, 512, 2, 512], P('frow', 'fcol')
- facet_update: float32 [2, 2048, 16384], P(None, 'frow', 'fcol')
All inputs are finite; a program needn't handle non-finite values.
Results may differ from a plain program's by a relative error of at most 0.0003.
Values sent between devices are 32-bit elements; how exact they have to be, the bound alone decides.
A program may use at most 64 MiB of HBM per device.

v0:
```python
import math

import jax
import jax.numpy as jnp
from jax import lax
from jax.sharding import PartitionSpec as P

SG = 512
MAXB = 64


HIGH = lax.Precision.HIGHEST


def table(first, count, anchor, length, modulus):
    freqs = (first + jnp.arange(count, dtype=jnp.int32)) % modulus
    coords = anchor + jnp.arange(length, dtype=jnp.int32)
    phase = freqs[:, None] * coords[None, :] % modulus
    angle = phase.astype(jnp.float32) * jnp.float32(2.0 * math.pi / modulus)
    scale = jnp.float32(1.0 / math.sqrt(modulus))
    return (jnp.cos(angle) * scale, jnp.sin(angle) * scale)


def table_batch(firsts, anchors, count, length, modulus):
    freqs = (firsts[..., None] + jnp.arange(count, dtype=jnp.int32)) % modulus
    coords = anchors[..., None] + jnp.arange(length, dtype=jnp.int32)
    phase = freqs[..., :, None] * coords[..., None, :] % modulus
    angle = phase.astype(jnp.float32) * jnp.float32(2.0 * math.pi / modulus)
    scale = jnp.float32(1.0 / math.sqrt(modulus))
    return (jnp.cos(angle) * scale, jnp.sin(angle) * scale)


def contract(form, left, right):
    return jnp.einsum(form, left, right, precision=HIGH)


def per_device(facets, column_start, subgrid_start, vis_count, vis_row, vis_weight):
    row_index = lax.axis_index("frow")
    col_index = lax.axis_index("fcol")
    row_devices = lax.axis_size("frow")
    col_devices = lax.axis_size("fcol")
    height, width = (facets.shape[1], facets.shape[2])
    rows_total = height * row_devices
    cols_total = width * col_devices
    sub_owned = vis_count.shape[0]
    col_local = SG // col_devices
    real_part, imag_part = (facets[0], facets[1])
    col_cos, col_sin = table(
        column_start[0], col_local * lax.axis_size("fcol"), col_index * width, width, cols_total
    )
    strip_re = contract("qy,xy->qx", col_cos, real_part) + contract("qy,xy->qx", col_sin, imag_part)
    strip_im = contract("qy,xy->qx", col_cos, imag_part) - contract("qy,xy->qx", col_sin, real_part)
    strip = lax.psum_scatter(
        jnp.stack([strip_re, strip_im], 1), "fcol", scatter_dimension=0, tiled=True
    )
    anchors = jnp.zeros((sub_owned * lax.axis_size("frow"),), jnp.int32) + row_index * height
    row_cos, row_sin = table_batch(subgrid_start, anchors, SG, height, rows_total)
    sub_re = contract("qx,spx->sqp", strip[:, 0], row_cos) + contract(
        "qx,spx->sqp", strip[:, 1], row_sin
    )
    sub_im = contract("qx,spx->sqp", strip[:, 1], row_cos) - contract(
        "qx,spx->sqp", strip[:, 0], row_sin
    )
    subs = lax.psum_scatter(jnp.stack([sub_re, sub_im], 2), "frow", scatter_dimension=0, tiled=True)
    live = (jnp.arange(MAXB, dtype=jnp.int32)[None, :] < vis_count[:, None]).astype(jnp.float32)
    onehot = (vis_row[:, :, None] == jnp.arange(SG, dtype=jnp.int32)[None, None, :]).astype(
        jnp.float32
    )
    gain = 1.0 + contract("sbq,sbp->sqp", vis_weight * live[:, :, None], onehot)
    corrected = subs * gain[:, :, None, :]
    piece = lax.all_gather(corrected, "frow", axis=0, tiled=True)
    count = piece.shape[0]
    anchors = jnp.zeros((count,), jnp.int32) + row_index * height
    row_cos, row_sin = table_batch(subgrid_start, anchors, SG, height, rows_total)
    back_re = contract("mqp,mpx->qx", piece[:, :, 0], row_cos) - contract(
        "mqp,mpx->qx", piece[:, :, 1], row_sin
    )
    back_im = contract("mqp,mpx->qx", piece[:, :, 1], row_cos) + contract(
        "mqp,mpx->qx", piece[:, :, 0], row_sin
    )
    back = jnp.stack([back_re, back_im], 1)
    piece = lax.all_gather(back, "fcol", axis=0, tiled=True)
    col_cos, col_sin = table(column_start[0], piece.shape[0], col_index * width, width, cols_total)
    image_re = contract("qx,qy->xy", piece[:, 0], col_cos) - contract(
        "qx,qy->xy", piece[:, 1], col_sin
    )
    image_im = contract("qx,qy->xy", piece[:, 1], col_cos) + contract(
        "qx,qy->xy", piece[:, 0], col_sin
    )
    facet_update = jnp.stack([image_re, image_im])
    return (corrected, facet_update)


def solution(mesh):
    return jax.shard_map(
        per_device,
        mesh=mesh,
        in_specs=(
            P(None, "frow", "fcol"),
            P(),
            P(),
            P("frow"),
            P("frow", None),
            P("frow", None, "fcol"),
        ),
        out_specs=(P("frow", "fcol", None, None), P(None, "frow", "fcol")),
        check_vma=False,
    )
```

profile of v0, /device:TPU:1, one launch (start us, length us, event | category | flops | bytes accessed | tf_op | source)
XLA Modules:
  0.0 582.3 jit_solution(18072297512777448642)
XLA Ops:
  7.2 0.0 reduce-scatter.5.cloned.1.call-start
  7.9 0.0 copy-start.4
  7.9 10.5 %fusion.33 = f32[512,128]{1,0:T(8,128)S(1)} fusion(s32[1024]{0:T(1024)S(1)} %iota_add_fusion, s32[512]{0:T(512)S(1)} %add_select_fusion.3, f32[2,128,1024]{2,1,0:T(8,128)} %param.6), kind=kOutput, calls=%fused_computation.40 | convolution fusion | flops 813170688 | bytes 792576 | tf_op jit(solution)/shard_map/qy,xy->qx/dot_general | solution.py:34
  18.4 0.0 copy-done.4
  18.4 9.7 %fusion.32 = f32[512,128]{1,0:T(8,128)S(1)} fusion(s32[1024]{0:T(1024)S(1)} %iota_add_fusion, s32[512]{0:T(512)S(1)} %add_select_fusion.3, f32[2,128,1024]{2,1,0:T(8,128)S(1)} %copy-done.4), kind=kOutput, calls=%fused_computation.39 | convolution fusion | flops 813170688 | bytes 792576 | tf_op jit(solution)/shard_map/qy,xy->qx/dot_general | solution.py:34
  28.1 9.6 %fusion.47 = f32[512,1,128]{2,0,1:T(8,128)S(1)} fusion(f32[512,128]{1,0:T(8,128)S(1)} %fusion.33, s32[1024]{0:T(1024)S(1)} %iota_add_fusion, s32[512]{0:T(512)S(1)} %add_select_fusion.3, f32[2,128,1024]{2,1,0:T(8,128)S(1)} %copy-done.4), kind=kOutput, calls=%fused_computation.54 | convolution fusion | flops 813236224 | bytes 1054720 | tf_op jit(solution)/shard_map/qy,xy->qx/dot_general | solution.py:34
  37.8 0.0 copy-start.1
  37.8 9.6 %fusion.49 = f32[512,1,128]{2,0,1:T(8,128)S(1)} fusion(f32[512,128]{1,0:T(8,128)S(1)} %fusion.32, s32[1024]{0:T(1024)S(1)} %iota_add_fusion, s32[512]{0:T(512)S(1)} %add_select_fusion.3, f32[2,128,1024]{2,1,0:T(8,128)S(1)} %copy-done.4), kind=kOutput, calls=%fused_computation.56 | convolution fusion | flops 813236224 | bytes 1054720 | tf_op jit(solution)/shard_map/qy,xy->qx/dot_general | solution.py:34
  47.5 0.8 pad_maximum_fusion.2
  48.3 0.0 reduce-scatter.5.cloned.1.call-update
  48.3 0.0 all-reduce.3.cloned.1.call-start
  48.4 0.0 copy-done.1
  48.4 0.1 add_select_fusion.2
  48.5 75.2 %reduce-scatter.5.cloned.1.call-done = f32[32,2,128]{2,0,1:T(8,128)} async-done(((f32[512,2,128]{2,0,1:T(8,128)}), f32[32,2,128]{2,0,1:T(8,128)}) %reduce-scatter.5.cloned.1.call-update) | async-done | bytes 32784 | tf_op jit(solution)/shard_map/reduce_scatter | solution.py:53
  123.7 0.0 copy-start.5
  123.7 21.4 %fusion.6 = f32[16,512,32]{1,2,0:T(8,128)S(1)} fusion(s32[128]{0:T(128)S(1)} %iota_add_fusion.1, s32[16,512]{1,0:T(8,128)S(1)} %add_select_fusion.2, f32[32,2,128]{2,0,1:T(8,128)} %reduce-scatter.5.cloned.1.call-done), kind=kOutput, calls=%fused_computation.18 | convolution fusion | flops 418381824 | bytes 1098240 | tf_op jit(solution)/shard_map/qx,spx->sqp/dot_general | solution.py:34
  145.1 0.0 copy-done.5
  145.1 20.6 %fusion.5 = f32[16,512,32]{1,2,0:T(8,128)S(1)} fusion(s32[128]{0:T(128)S(1)} %iota_add_fusion.1, s32[16,512]{1,0:T(8,128)S(1)} %add_select_fusion.2, f32[32,2,128]{2,0,1:T(8,128)S(1)} %copy-done.5), kind=kOutput, calls=%fused_computation.17 | convolution fusion | flops 418381824 | bytes 1098240 | tf_op jit(solution)/shard_map/qx,spx->sqp/dot_general | solution.py:34
  165.7 20.8 %fusion.39 = f32[16,32,1,512]{3,1,0,2:T(8,128)S(1)} fusion(f32[16,512,32]{1,2,0:T(8,128)S(1)} %fusion.6, s32[128]{0:T(128)S(1)} %iota_add_fusion.1, s32[16,512]{1,0:T(8,128)S(1)} %add_select_fusion.2, f32[32,2,128]{2,0,1:T(8,128)S(1)} %copy-done.5), kind=kOutput, calls=%fused_computation.46 | convolution fusion | flops 418643968 | bytes 2146816 | tf_op jit(solution)/shard_map/qx,spx->sqp/dot_general | solution.py:34
  186.5 20.8 %fusion.41 = f32[16,32,1,512]{3,1,0,2:T(8,128)S(1)} fusion(f32[16,512,32]{1,2,0:T(8,128)S(1)} %fusion.5, s32[128]{0:T(128)S(1)} %iota_add_fusion.1, s32[16,512]{1,0:T(8,128)S(1)} %add_select_fusion.2, f32[32,2,128]{2,0,1:T(8,128)S(1)} %copy-done.5), kind=kOutput, calls=%fused_computation.48 | convolution fusion | flops 418643968 | bytes 2146816 | tf_op jit(solution)/shard_map/qx,spx->sqp/dot_general | solution.py:34
  207.3 1.5 pad_maximum_fusion
  208.8 0.0 copy-start.6
  208.8 0.0 copy-start
  208.8 0.0 copy-start.2
  208.8 0.0 all-reduce.3.cloned.1.call-update
  208.8 0.4 all-gather.2.cloned.1.call-start
  209.9 0.0 copy-done.6
  209.9 0.6 dynamic-slice
  210.5 0.0 copy-done
  210.5 0.0 copy-done.2
  210.5 0.2 convolution_add_fusion
  210.8 136.2 %all-reduce.3.cloned.1.call-done = f32[16,32,2,512]{3,1,0,2:T(8,128)} async-done(((f32[16,32,2,512]{3,1,0,2:T(8,128)}), f32[16,32,2,512]{3,1,0,2:T(8,128)}) %all-reduce.3.cloned.1.call-update) | async-done | bytes 2097168
  347.0 2.2 dynamic-slice_multiply_fusion
  349.2 0.0 all-gather.2.cloned.1.call-update
  349.2 1.7 copy.10
  350.9 69.5 %all-gather.2.cloned.1.call-done = f32[16,32,2,512]{3,1,0,2:T(8,128)} async-done(((f32[1,32,2,512]{3,1,0,2:T(8,128)}), f32[16,32,2,512]{3,1,0,2:T(8,128)}) %all-gather.2.cloned.1.call-update) | async-done | bytes 2097168 | tf_op jit(solution)/shard_map/all_gather | solution.py:71
  420.4 0.0 copy-start.3
  420.4 22.2 %fusion.50 = f32[32,128]{1,0:T(8,128)S(1)} fusion(s32[128]{0:T(128)S(1)} %iota_add_fusion.1, s32[16,512]{1,0:T(8,128)S(1)} %add_select_fusion.2, f32[16,32,2,512]{3,1,0,2:T(8,128)} %all-gather.2.cloned.1.call-done), kind=kOutput, calls=%fused_computation.58 | convolution fusion | flops 418381824 | bytes 1098240 | tf_op jit(solution)/shard_map/mqp,mpx->qx/dot_general | solution.py:34
  442.6 0.0 copy-done.3
  442.6 19.3 %fusion.51 = f32[32,128]{1,0:T(8,128)S(1)} fusion(s32[128]{0:T(128)S(1)} %iota_add_fusion.1, s32[16,512]{1,0:T(8,128)S(1)} %add_select_fusion.2, f32[16,32,2,512]{3,1,0,2:T(8,128)S(1)} %copy-done.3), kind=kOutput, calls=%fused_computation.59 | convolution fusion | flops 418381824 | bytes 1098240 | tf_op jit(solution)/shard_map/mqp,mpx->qx/dot_general | solution.py:34
  461.9 19.2 %fusion.57 = f32[32,1,128]{2,0,1:T(8,128)S(1)} fusion(f32[32,128]{1,0:T(8,128)S(1)} %fusion.50, s32[128]{0:T(128)S(1)} %iota_add_fusion.1, s32[16,512]{1,0:T(8,128)S(1)} %add_select_fusion.2, f32[16,32,2,512]{3,1,0,2:T(8,128)S(1)} %copy-done.3), kind=kOutput, calls=%fused_computation.65 | convolution fusion | flops 418385920 | bytes 1114624 | tf_op jit(solution)/shard_map/mqp,mpx->qx/dot_general | solution.py:34
  481.0 19.2 %fusion.55 = f32[32,1,128]{2,0,1:T(8,128)S(1)} fusion(f32[32,128]{1,0:T(8,128)S(1)} %fusion.51, s32[128]{0:T(128)S(1)} %iota_add_fusion.1, s32[16,512]{1,0:T(8,128)S(1)} %add_select_fusion.2, f32[16,32,2,512]{3,1,0,2:T(8,128)S(1)} %copy-done.3), kind=kOutput, calls=%fused_computation.63 | convolution fusion | flops 418385920 | bytes 1114624 | tf_op jit(solution)/shard_map/mqp,mpx->qx/dot_general | solution.py:34
  500.2 37.6 %all_gather.7 = f32[512,2,128]{2,0,1:T(8,128)S(1)} all-gather(f32[32,2,128]{2,0,1:T(8,128)S(1)} %pad_maximum_fusion.3), channel_id=1, replica_groups=mesh['frow'=16,'fcol'=16] {'fcol'}, dimensions={0}, use_global_device_ids=true | all-gather | bytes 557056 | tf_op jit(solution)/shard_map/all_gather | solution.py:82
  537.8 9.0 %fusion.31 = f32[128,1024]{1,0:T(8,128)S(1)} fusion(s32[1024]{0:T(1024)S(1)} %iota_add_fusion, s32[512]{0:T(512)S(1)} %add_select_fusion.3, f32[512,2,128]{2,0,1:T(8,128)S(1)} %all_gather.7), kind=kOutput, calls=%fused_computation.38 | convolution fusion | flops 813170688 | bytes 792576 | tf_op jit(solution)/shard_map/qx,qy->xy/dot_general | solution.py:34
  546.8 9.4 %fusion.30 = f32[128,1024]{1,0:T(8,128)S(1)} fusion(s32[1024]{0:T(1024)S(1)} %iota_add_fusion, s32[512]{0:T(512)S(1)} %add_select_fusion.3, f32[512,2,128]{2,0,1:T(8,128)S(1)} %all_gather.7), kind=kOutput, calls=%fused_computation.37 | convolution fusion | flops 813170688 | bytes 792576 | tf_op jit(solution)/shard_map/qx,qy->xy/dot_general | solution.py:34
  556.2 9.2 %fusion.43 = f32[1,128,1024]{2,1,0:T(8,128)S(1)} fusion(f32[128,1024]{1,0:T(8,128)S(1)} %fusion.31, s32[1024]{0:T(1024)S(1)} %iota_add_fusion, s32[512]{0:T(512)S(1)} %add_select_fusion.3, f32[512,2,128]{2,0,1:T(8,128)S(1)} %all_gather.7), kind=kOutput, calls=%fused_computation.50 | convolution fusion | flops 813301760 | bytes 1316864 | tf_op jit(solution)/shard_map/qx,qy->xy/dot_general | solution.py:34
  565.4 9.1 %fusion.45 = f32[1,128,1024]{2,1,0:T(8,128)S(1)} fusion(f32[128,1024]{1,0:T(8,128)S(1)} %fusion.30, s32[1024]{0:T(1024)S(1)} %iota_add_fusion, s32[512]{0:T(512)S(1)} %add_select_fusion.3, f32[512,2,128]{2,0,1:T(8,128)S(1)} %all_gather.7), kind=kOutput, calls=%fused_computation.52 | convolution fusion | flops 813301760 | bytes 1316864 | tf_op jit(solution)/shard_map/qx,qy->xy/dot_general | solution.py:34
  574.5 1.1 pad_maximum_fusion.1
  (5 shorter events, 0.0 us)
Async XLA Ops:
  7.2 116.5 %reduce-scatter.5.cloned.1.call-start = ((), (), s32[]{:S(2)}) async-start(), calls=%async_computation.1 | async-start | bytes 557056 | tf_op jit(solution)/shard_map/reduce_scatter | solution.py:53
  7.9 10.5 %copy-start.4 = (f32[2,128,1024]{2,1,0:T(8,128)S(1)}, f32[2,128,1024]{2,1,0:T(8,128)}, u32[]{:S(2)}) copy-start(f32[2,128,1024]{2,1,0:T(8,128)} %param.6) | copy-start | bytes 3145732
  37.8 10.6 %copy-start.1 = (s32[16]{0:T(128)S(1)}, s32[16]{0:T(128)}, u32[]{:S(2)}) copy-start(s32[16]{0:T(128)} %param.8) | copy-start | bytes 196
  48.3 298.7 %all-reduce.3.cloned.1.call-start = ((), (), s32[]{:S(2)}) async-start(), calls=%async_computation.3 | async-start | bytes 4194304
  123.7 21.4 %copy-start.5 = (f32[32,2,128]{2,0,1:T(8,128)S(1)}, f32[32,2,128]{2,0,1:T(8,128)}, u32[]{:S(2)}) copy-start(f32[32,2,128]{2,0,1:T(8,128)} %reduce-scatter.5.cloned.1.call-done) | copy-start | bytes 98308
  208.8 1.1 copy-start.6
  208.8 1.7 copy-start
  208.8 1.7 copy-start.2
  208.8 211.6 %all-gather.2.cloned.1.call-start = ((), (), s32[]{:S(2)}) async-start(), calls=%async_computation.2 | async-start | bytes 2228224 | tf_op jit(solution)/shard_map/all_gather | solution.py:71
  420.4 22.2 %copy-start.3 = (f32[16,32,2,512]{3,1,0,2:T(8,128)S(1)}, f32[16,32,2,512]{3,1,0,2:T(8,128)}, u32[]{:S(2)}) copy-start(f32[16,32,2,512]{3,1,0,2:T(8,128)} %all-gather.2.cloned.1.call-done) | copy-start | bytes 6291460
Sparse Core Ops, SparseCore 0:
  48.4 75.2 reduce-scatter.4
  208.9 137.9 all-reduce.2
  349.3 71.0 all-gather.1
where the time goes:
time: 591 us; the launch traced here: 582 us
  waiting for transfers between devices  281 us (48%)
  matrix products  240 us (41%)
  blocking collectives  37.6 us (6%)
  between operations  15.5 us (3%)
    dot_general x17, matrix products, contract(): return jnp.einsum(form, left, right, precision=HIGH)  240 us
    unnamed x4, waiting for transfers between devices  136 us
    reduce_scatter x1, waiting for transfers between devices, per_device(): lax.psum_scatter(jnp.stack([strip_re, strip_im], 1), 'fcol', scatter_dime...  75.2 us
    all_gather x1, waiting for transfers between devices, per_device(): piece = lax.all_gather(corrected, 'frow', axis=0, tiled=True)  69.5 us
    all_gather x1, blocking collectives, per_device(): piece = lax.all_gather(back, 'fcol', axis=0, tiled=True)  37.6 us
  transfers between devices with their start and end apart: 3, of which 3 were waited for; matrix products, arithmetic and copies ran while one was open for 0% of the time, Pallas kernels for 0%

commit v1 on v0

v1 whole, which is shorter than its diff:
```python
import math

import jax
import jax.numpy as jnp
from jax import lax
from jax.experimental import pallas as pl
from jax.experimental.pallas import tpu as pltpu
from jax.sharding import PartitionSpec as P

SG = 512
MAXB = 64
NR = 16
NC = 16
N1 = 2048
N2 = 16384
LW = 1024
LH = 128

F32 = jnp.float32
BF16 = jnp.bfloat16
I32 = jnp.int32
MESH = pl.DeviceIdType.MESH


def iota(shape, axis):
    return lax.broadcasted_iota(I32, shape, axis)


def sincos(t, lg):
    q = (t + (1 << (lg - 3))) >> (lg - 2)
    r = t - (q << (lg - 2))
    th = r.astype(F32) * F32(2.0 * math.pi / (1 << lg))
    z = th * th
    s = th * (1.0 + z * (-1.0 / 6 + z * (1.0 / 120 + z * (-1.0 / 5040 + z * (1.0 / 362880)))))
    c = 1.0 + z * (-0.5 + z * (1.0 / 24 + z * (-1.0 / 720 + z * (1.0 / 40320))))
    odd = (q & 1) == 1
    cc = jnp.where(odd, s, c)
    ss = jnp.where(odd, c, s)
    return (
        jnp.where(((q + 1) & 2) != 0, -cc, cc),
        jnp.where((q & 2) != 0, -ss, ss),
    )


def split(x):
    hi = x.astype(BF16)
    return hi, (x - hi.astype(F32)).astype(BF16)


def dot(a, b):
    return lax.dot_general(a, b, (((1,), (0,)), ((), ())), preferred_element_type=F32)


def dot_t(a, b):
    return lax.dot_general(a, b, (((1,), (1,)), ((), ())), preferred_element_type=F32)


def dot3(a, b):
    ah, al = split(a)
    bh, bl = split(b)
    return dot(ah, bh) + (dot(ah, bl) + dot(al, bh))


def kernel(
    cs_ref, ss_ref, vc_ref, vr_ref, vw_ref, fac_hbm,
    cor_hbm, img_hbm,
    xv, rh, rl, arow, thi, tlo, part,
    rec_k, snd_h, rec_h, snd_y, rec_y,
    snd_a, rec_a, d1, twc, tws, gai_s, gai_r, g_s, g_r,
    snd_b, rec_b, agb, cor_v, img_v,
    load_sem, out_sem, ks_sem, kr_sem, hs_sem, hr_sem, ys_sem, yr_sem,
    gs_sem, gr_sem, as_sem, ar_sem, cs_sem, cr_sem, bs_sem, br_sem,
    ays_sem, ayr_sem, ahs_sem, ahr_sem, aks_sem, akr_sem,
):
    r = lax.axis_index("frow")
    c = lax.axis_index("fcol")
    y = c // 4
    h = (c // 2) % 2
    k = c % 2
    dev_k = (r, c + 1 - 2 * k)
    dev_h = (r, c + 2 - 4 * h)
    y_peers = [(y + d) % 4 for d in range(4)]
    dev_y = [(r, yp * 4 + c % 4) for yp in y_peers]
    r_peers = [(r + d) % NR for d in range(NR)]
    dev_r = [(rp, c) for rp in r_peers]

    def remote(src, dst, ssem, rsem, dev):
        return pltpu.make_async_remote_copy(
            src_ref=src, dst_ref=dst, send_sem=ssem, recv_sem=rsem,
            device_id=dev, device_id_type=MESH,
        )

    barrier = pltpu.get_barrier_semaphore()
    for dev in [dev_k, dev_h] + dev_y[1:] + dev_r[1:]:
        pl.semaphore_signal(barrier, inc=1, device_id=dev, device_id_type=MESH)

    load = pltpu.make_async_copy(fac_hbm, xv, load_sem)
    load.start()

    f = cs_ref[0]
    off = c * LW
    coord = off + iota((32, LW), 1)
    g = iota((32, LW), 0)
    qbase = ((g >> 1) & 3) * 128 + ((g >> 3) & 1) * 64 + (g >> 4) * 32 + (g & 1) * 16
    t = (((f + qbase) & (N2 - 1)) * coord) & (N2 - 1)
    ac, asn = sincos(t, 14)
    arow[0] = ac * F32(1.0 / math.sqrt(N2))
    arow[1] = asn * F32(1.0 / math.sqrt(N2))
    bc, bs = sincos((iota((16, LW), 0) * (off + iota((16, LW), 1))) & (N2 - 1), 14)

    @pl.loop(0, 32)
    def _(i):
        ca = arow[0, pl.ds(i, 1), :]
        sa = arow[1, pl.ds(i, 1), :]
        rows = pl.ds(pl.multiple_of(i * 16, 16), 16)
        th, tl = split(ca * bc - sa * bs)
        thi[0, rows, :] = th
        tlo[0, rows, :] = tl
        th, tl = split(sa * bc + ca * bs)
        thi[1, rows, :] = th
        tlo[1, rows, :] = tl

    load.wait()
    xr = xv[0]
    xi = xv[1]
    xrh, xrl = split(xr)
    xih, xil = split(xi)
    rh[0, 0:LH] = xrh
    rh[0, LH:] = xih
    rh[1, 0:LH] = xih
    rh[1, LH:] = -xrh
    rl[0, 0:LH] = xrl
    rl[0, LH:] = xil
    rl[1, 0:LH] = xil
    rl[1, LH:] = -xrl

    def strip_half(kk):
        rows = pl.ds(pl.multiple_of(kk * 256, 256), 256)
        acc = None
        for m in range(2):
            a = thi[m, rows, :]
            b = tlo[m, rows, :]
            s = dot_t(a, rh[m]) + (dot_t(a, rl[m]) + dot_t(b, rh[m]))
            acc = s if acc is None else acc + s
        for hh in range(2):
            for yy in range(4):
                base = (hh * 4 + yy) * 32
                for p in range(2):
                    part[kk, hh, yy, p] = acc[base : base + 32, p * LH : (p + 1) * LH]

    strip_half(1 - k)
    pl.semaphore_wait(barrier, 20)
    k_copy = remote(part.at[1 - k], rec_k, ks_sem, kr_sem, dev_k)
    k_copy.start()
    strip_half(k)

    rows_l = vr_ref[...]
    diag = iota((MAXB, MAXB), 0) == iota((MAXB, MAXB), 1)
    row_c = jnp.sum(
        jnp.where(diag, jnp.broadcast_to(rows_l, (MAXB, MAXB)).astype(F32), 0.0), axis=1, keepdims=True
    )
    row_c = row_c.astype(I32)
    wide = NR * 128
    lane = iota((32, wide), 1)
    sel = (iota((32, wide), 0) == ((lane >> 6) & 1) * 16 + (lane >> 7)).astype(F32).astype(BF16)
    w = vw_ref[0]
    w1 = w.astype(BF16)
    rest = w - w1.astype(F32)
    w2 = rest.astype(BF16)
    w3 = (rest - w2.astype(F32)).astype(BF16)
    wide_w = (dot(w1, sel) + dot(w2, sel)) + dot(w3, sel)
    wide_w = jnp.where((row_c >> 4) == (iota((MAXB, wide), 1) & 31), wide_w, 0.0)
    wh, wl = split(wide_w)
    low = jnp.broadcast_to(rows_l, (16, MAXB)) & 15
    lhs = ((low == iota((16, MAXB), 0)) & (iota((16, MAXB), 1) < vc_ref[0])).astype(F32).astype(BF16)
    gain = 1.0 + (dot(lhs, wh) + dot(lhs, wl))
    for i in range(NR):
        gai_s[i] = gain[:, i * 128 : (i + 1) * 128]

    k_copy.wait_recv()
    for yy in range(4):
        snd_h[yy] = part[k, 1 - h, yy] + rec_k[1 - h, yy]
    h_copy = remote(snd_h, rec_h, hs_sem, hr_sem, dev_h)
    h_copy.start()
    g_copies = [
        remote(gai_s.at[r_peers[d]], gai_r.at[r], gs_sem.at[d], gr_sem.at[d], dev_r[d])
        for d in range(1, NR)
    ]
    for cp in g_copies:
        cp.start()
    gai_r[r] = gai_s[r]

    mu = iota((16, 128), 0)
    lb = iota((16, 128), 1)

    @pl.loop(0, NR)
    def _(s):
        kf = (ss_ref[s] + mu) & (N1 - 1)
        rows = pl.ds(pl.multiple_of(s * 16, 16), 16)
        cc, sn = sincos((kf * lb) & (N1 - 1), 11)
        twc[rows, :] = cc * F32(1.0 / math.sqrt(N1))
        tws[rows, :] = sn * F32(1.0 / math.sqrt(N1))
        ca, sa = sincos((kf * (lb & 15)) & 15, 4)
        pi = (lb >> 4) & 1
        blk = lb >> 5
        for po in range(2):
            v = jnp.where(pi == 0, ca, sa) if po == 0 else jnp.where(pi == 0, -sa, ca)
            hi = v.astype(BF16).astype(F32)
            v = jnp.where(blk < 2, hi, jnp.where(blk == 2, v - hi, 0.0))
            d1[po, rows, :] = v.astype(BF16)

    row = iota((512, 128), 0)
    col = iota((512, 128), 1)
    cc, sn = sincos(((row & 127) * (col & 31)) & 127, 7)
    pin = (row >> 7) & 1
    pout = (col >> 5) & 1
    same = (row >> 8) == (col >> 6)
    e3 = jnp.where(pin == pout, cc, jnp.where(pin == 1, sn, -sn))
    e3h, e3l = split(jnp.where(same, e3, 0.0))
    row = iota((128, 512), 0)
    col = iota((128, 512), 1)
    cc, sn = sincos(((col & 127) * (row & 31)) & 127, 7)
    pin = (row >> 5) & 1
    pout = (col >> 7) & 1
    same = (col >> 8) == (row >> 6)
    e4 = jnp.where(pin == pout, cc, jnp.where(pin == 1, -sn, sn))
    e4h, e4l = split(jnp.where(same, e4, 0.0))
    lane = iota((16, 256), 1)
    first = jnp.zeros((16, 256), I32)
    for s in range(NR):
        first = jnp.where((lane >> 4) == s, ss_ref[s], first)
    ca, sa = sincos(((first + (lane & 15)) * iota((16, 256), 0)) & 15, 4)
    d2 = jnp.concatenate(
        [jnp.concatenate([ca, -sa], axis=1), jnp.concatenate([sa, ca], axis=1)], axis=0
    )
    d2h, d2l = split(d2)

    h_copy.wait_recv()
    for yy in range(4):
        snd_y[yy] = (part[k, h, yy] + rec_k[h, yy]) + rec_h[yy]
    y_copies = [
        remote(snd_y.at[y_peers[d]], rec_y.at[d - 1], ys_sem.at[d], yr_sem.at[d], dev_y[d])
        for d in range(1, 4)
    ]
    for cp in y_copies:
        cp.start()
    for cp in y_copies:
        cp.wait_recv()
    strip = (snd_y[y] + rec_y[0]) + (rec_y[1] + rec_y[2])
    for p in range(2):
        for q in range(2):
            snd_a[:, p * 2 + q, :] = strip[p, q * 16 : (q + 1) * 16, :]
    a_copies = [
        remote(snd_a.at[r_peers[d]], rec_a.at[r], as_sem.at[d], ar_sem.at[d], dev_r[d])
        for d in range(1, NR)
    ]
    for cp in a_copies:
        cp.start()
    rec_a[r] = snd_a[r]
    for cp in a_copies:
        cp.wait_recv()
    for cp in g_copies:
        cp.wait_recv()

    v = jnp.concatenate(
        [jnp.concatenate([rec_a[:, p * 2 + q, :] for q in range(2)], axis=1) for p in range(2)], axis=0
    )
    vh, vl = split(v)
    stack = jnp.concatenate([vh, vl, vh, jnp.zeros_like(vh)], axis=0)
    zre = dot(d1[0], stack)
    zim = dot(d1[1], stack)
    tc = twc[...]
    ts = tws[...]
    cols = []
    for q in range(2):
        re = zre[:, q * 128 : (q + 1) * 128]
        im = zim[:, q * 128 : (q + 1) * 128]
        cols += [re * tc + im * ts, im * tc - re * ts]
    zh, zl = split(jnp.concatenate(cols, axis=1))
    sub = dot(zh, e3h) + (dot(zh, e3l) + dot(zl, e3h))
    grid = sub * gai_r[...].reshape(256, 128)
    g_s[...] = grid.reshape(NR, 16, 128)
    c_copies = [
        remote(g_s.at[r_peers[d]], g_r.at[r], cs_sem.at[d], cr_sem.at[d], dev_r[d])
        for d in range(1, NR)
    ]
    for cp in c_copies:
        cp.start()
    gh, gl = split(grid)
    vv = dot(gh, e4h) + (dot(gh, e4l) + dot(gl, e4h))
    res = []
    ims = []
    for q in range(2):
        re = vv[:, q * 256 : q * 256 + 128]
        im = vv[:, q * 256 + 128 : q * 256 + 256]
        res.append(re * tc - im * ts)
        ims.append(im * tc + re * ts)
    both = jnp.concatenate([jnp.concatenate(res, axis=1), jnp.concatenate(ims, axis=1)], axis=0)
    bh, bl = split(both)
    back = dot(d2h, bh) + (dot(d2h, bl) + dot(d2l, bh))
    for p in range(2):
        for q in range(2):
            snd_b[:, p * 2 + q, :] = back[p * 16 : (p + 1) * 16, q * 128 : (q + 1) * 128]
    b_copies = [
        remote(snd_b.at[r_peers[d]], rec_b.at[r], bs_sem.at[d], br_sem.at[d], dev_r[d])
        for d in range(1, NR)
    ]
    for cp in b_copies:
        cp.start()
    rec_b[r] = snd_b[r]
    g_r[r] = g_s[r]
    for cp in b_copies:
        cp.wait_recv()
    for p in range(2):
        for q in range(2):
            agb[k, h, y, p, q * 16 : (q + 1) * 16, :] = rec_b[:, p * 2 + q, :]

    mine = agb.at[k, h, y]
    ay = [
        remote(mine, mine, ays_sem.at[d], ayr_sem.at[d], dev_y[d]) for d in range(1, 4)
    ]
    from_y = [agb.at[k, h, (y + 4 - d) % 4] for d in range(4)]
    ah = [remote(from_y[d], from_y[d], ahs_sem.at[d], ahr_sem.at[d], dev_h) for d in range(4)]
    ak = [remote(from_y[d], from_y[d], aks_sem.at[d], akr_sem.at[d], dev_k) for d in range(4)]
    oth = agb.at[k, 1 - h]
    ak_h = remote(oth, oth, aks_sem.at[4], akr_sem.at[4], dev_k)
    for cp in ay:
        cp.start()
    ah[0].start()
    ak[0].start()
    for d in range(1, 4):
        in_y = remote(from_y[d], from_y[d], ays_sem.at[d], ayr_sem.at[d], dev_y[d])
        in_y.wait_recv()
        ah[d].start()
        ak[d].start()

    for cp in c_copies:
        cp.wait_recv()
    lane = iota((128, SG), 1)
    rowi = iota((128, SG), 0)
    gath = g_r[...].reshape(256, 128)
    g1 = gath.astype(BF16)
    rest = gath - g1.astype(F32)
    g2 = rest.astype(BF16)
    g3 = (rest - g2.astype(F32)).astype(BF16)
    keep = (iota((256, SG), 0) & 15) == (iota((256, SG), 1) & 15)
    for q in range(2):
        for p in range(2):
            ex = (rowi == (q * 2 + p) * 32 + (lane >> 4)).astype(F32).astype(BF16)
            wide_g = (dot(g1, ex) + dot(g2, ex)) + dot(g3, ex)
            wide_g = jnp.where(keep, wide_g, 0.0)
            cor_v[0, q * 16 : (q + 1) * 16, p, :] = jnp.sum(wide_g.reshape(16, 16, SG), axis=1)
    cor_out = pltpu.make_async_copy(cor_v, cor_hbm, out_sem.at[4])
    cor_out.start()

    for d in range(4):
        src = agb.at[k, 1 - h, (y + 4 - d) % 4]
        remote(src, src, ahs_sem.at[d], ahr_sem.at[d], dev_h).wait_recv()
    ak_h.start()
    for d in range(4):
        src = agb.at[1 - k, h, (y + 4 - d) % 4]
        remote(src, src, aks_sem.at[d], akr_sem.at[d], dev_k).wait_recv()
    src = agb.at[1 - k, 1 - h]
    remote(src, src, aks_sem.at[4], akr_sem.at[4], dev_k).wait_recv()

    bre = []
    bim = []
    for kk in range(2):
        for hh in range(2):
            for yy in range(4):
                bre.append(agb[kk, hh, yy, 0])
                bim.append(agb[kk, hh, yy, 1])
    re_t = jnp.concatenate(bre, axis=0).T
    im_t = jnp.concatenate(bim, axis=0).T
    l1h, l1l = split(jnp.concatenate([re_t, im_t], axis=0))
    l2h, l2l = split(jnp.concatenate([-im_t, re_t], axis=0))
    outs = []
    for n in range(4):
        cols = slice(n * 256, (n + 1) * 256)
        ch = thi[0, :, cols]
        cl = tlo[0, :, cols]
        sh = thi[1, :, cols]
        sl = tlo[1, :, cols]
        o = (dot(l1h, ch) + dot(l2h, sh)) + (
            (dot(l1l, ch) + dot(l2l, sh)) + (dot(l1h, cl) + dot(l2h, sl))
        )
        img_v[0, :, cols] = o[:LH]
        img_v[1, :, cols] = o[LH:]
        cp = pltpu.make_async_copy(img_v.at[:, :, cols], img_hbm.at[:, :, cols], out_sem.at[n])
        cp.start()
        outs.append(cp)

    for cp in [k_copy, h_copy, *y_copies, *g_copies, *a_copies, *c_copies, *b_copies, *ay, *ah, *ak, ak_h]:
        cp.wait_send()
    for cp in outs:
        cp.wait()
    cor_out.wait()


def per_device(facets, column_start, subgrid_start, vis_count, vis_row, vis_weight):
    dma = pltpu.SemaphoreType.DMA
    vm = pltpu.VMEM
    smem = pl.BlockSpec(memory_space=pltpu.SMEM)
    vmem = pl.BlockSpec(memory_space=pltpu.VMEM)
    anym = pl.BlockSpec(memory_space=pl.ANY)
    return pl.pallas_call(
        kernel,
        out_shape=(
            jax.ShapeDtypeStruct((1, 32, 2, SG), F32),
            jax.ShapeDtypeStruct((2, LH, LW), F32),
        ),
        in_specs=[smem, smem, smem, vmem, vmem, anym],
        out_specs=(anym, anym),
        scratch_shapes=[
            vm((2, LH, LW), F32),
            vm((2, 2 * LH, LW), BF16),
            vm((2, 2 * LH, LW), BF16),
            vm((2, 32, LW), F32),
            vm((2, SG, LW), BF16),
            vm((2, SG, LW), BF16),
            vm((2, 2, 4, 2, 32, LH), F32),
            vm((2, 4, 2, 32, LH), F32),
            vm((4, 2, 32, LH), F32),
            vm((4, 2, 32, LH), F32),
            vm((4, 2, 32, LH), F32),
            vm((3, 2, 32, LH), F32),
            vm((NR, 4, 128), F32),
            vm((NR, 4, 128), F32),
            vm((2, 256, 128), BF16),
            vm((256, 128), F32),
            vm((256, 128), F32),
            vm((NR, 16, 128), F32),
            vm((NR, 16, 128), F32),
            vm((NR, 16, 128), F32),
            vm((NR, 16, 128), F32),
            vm((NR, 4, 128), F32),
            vm((NR, 4, 128), F32),
            vm((2, 2, 4, 2, 32, LH), F32),
            vm((1, 32, 2, SG), F32),
            vm((2, LH, LW), F32),
            dma, dma((5,)), dma, dma, dma, dma, dma((4,)), dma((4,)),
            dma((NR,)), dma((NR,)), dma((NR,)), dma((NR,)), dma((NR,)), dma((NR,)), dma((NR,)), dma((NR,)),
            dma((4,)), dma((4,)), dma((4,)), dma((4,)), dma((5,)), dma((5,)),
        ],
        compiler_params=pltpu.CompilerParams(collective_id=0, has_side_effects=True),
    )(column_start, subgrid_start, vis_count, vis_row, vis_weight, facets)


def solution(mesh):
    return jax.shard_map(
        per_device,
        mesh=mesh,
        in_specs=(
            P(None, "frow", "fcol"),
            P(),
            P(),
            P("frow"),
            P("frow", None),
            P("frow", None, "fcol"),
        ),
        out_specs=(P("frow", "fcol", None, None), P(None, "frow", "fcol")),
        check_vma=False,
    )
```

time: 591 us -> 56.6 us (0.10); the launches traced: 582 us -> 56.4 us
  waiting for transfers between devices: 281 us -> 0 us
  matrix products: 240 us -> 0 us
  Pallas kernels: 0 us -> 49.1 us
  blocking collectives: 37.6 us -> 0 us
  between operations: 15.5 us -> 1.93 us
    dot_general x17 -> x0, matrix products: 240 us -> none  [contract(): return jnp.einsum(form, left, right, precision=HIGH)]
    unnamed x4 -> x0, waiting for transfers between devices: 136 us -> none
    reduce_scatter x1 -> x0, waiting for transfers between devices: 75.2 us -> none  [per_device(): lax.psum_scatter(jnp.stack([strip_re, strip_im], 1), 'fcol', scatter_dime...]
    all_gather x1 -> x0, waiting for transfers between devices: 69.5 us -> none  [per_device(): piece = lax.all_gather(corrected, 'frow', axis=0, tiled=True)]
    pallas_call x0 -> x1, Pallas kernels: none -> 49.1 us  [per_device(): pl.pallas_call(kernel, out_shape=(jax.ShapeDtypeStruct((1, 32, 2, SG), F3...]
    all_gather x1 -> x0, blocking collectives: 37.6 us -> none  [per_device(): piece = lax.all_gather(back, 'fcol', axis=0, tiled=True)]
  transfers between devices with their start and end apart: 3 -> 0, of which waited for: 3 -> 0; matrix products, arithmetic and copies ran while one was open for 0% -> 0% of each run, Pallas kernels for 0% -> 0%
where the time goes in v1:
time: 56.6 us; the launch traced here: 56.4 us
  Pallas kernels  49.1 us (87%)
  local copies, waits for them, and re-layouts  5.29 us (9%)
  between operations  1.93 us (3%)
    pallas_call x1, Pallas kernels, per_device(): pl.pallas_call(kernel, out_shape=(jax.ShapeDtypeStruct((1, 32, 2, SG), F3...  49.1 us
    unnamed x3, local copies, waits for them, and re-layouts  5.29 us

profile of v1, /device:TPU:1, one launch (start us, length us, event | category | flops | bytes accessed | tf_op | source)
XLA Modules:
  0.0 56.4 jit_solution(6190942182524422889)
XLA Ops:
  1.9 1.4 %copy.8.vw_ref = f32[1,64,32]{2,1,0:T(8,128)} copy(f32[1,64,32]{1,2,0:T(8,128)} %param.11) | data formatting | bytes 16384 | tf_op args[5]
  3.3 49.1 %shard_map.77 = (f32[1,32,2,512]{3,2,1,0:T(2,128)}, f32[2,128,1024]{2,1,0:T(8,128)}) custom-call(s32[1]{0:T(128)S(6)} %copy.11.cs_ref, s32[16]{0:T(128)} %ss_ref.1, s32[1]{0:T(128)S(6)} %copy.12.vc_ref, s32[1,64]{1,0:T(1,128)} %vr_ref.1, f32[1,64,32]{2,1,0:T(8,128)} %copy.8.vw_ref, f32[2,128,1024]{2,1,0:T(8,128)} %fac_hbm.1), custom_call_target="tpu_custom_call" | custom-call | tf_op jit(solution)/shard_map/pallas_call | solution.py:406
  52.5 1.6 %copy.13 = f32[1,32,2,512]{3,2,1,0:T(2,128)} copy(f32[1,32,2,512]{3,2,1,0:T(2,128)} %get-tuple-element.4) | data formatting | bytes 262144
  54.1 2.3 %copy.14 = f32[2,128,1024]{2,1,0:T(8,128)} copy(f32[2,128,1024]{2,1,0:T(8,128)} %get-tuple-element.5) | data formatting | bytes 2097152

commit v2 on v1

v2 whole, which is shorter than its diff:
```python
import math

import jax
import jax.numpy as jnp
from jax import lax
from jax.experimental import pallas as pl
from jax.experimental.pallas import tpu as pltpu
from jax.sharding import PartitionSpec as P

SG = 512
MAXB = 64
NR = 16
NC = 16
N1 = 2048
N2 = 16384
LW = 1024
LH = 128

F32 = jnp.float32
BF16 = jnp.bfloat16
I32 = jnp.int32
MESH = pl.DeviceIdType.MESH


def iota(shape, axis):
    return lax.broadcasted_iota(I32, shape, axis)


def sincos(t, lg):
    q = (t + (1 << (lg - 3))) >> (lg - 2)
    r = t - (q << (lg - 2))
    th = r.astype(F32) * F32(2.0 * math.pi / (1 << lg))
    z = th * th
    s = th * (1.0 + z * (-1.0 / 6 + z * (1.0 / 120 + z * (-1.0 / 5040 + z * (1.0 / 362880)))))
    c = 1.0 + z * (-0.5 + z * (1.0 / 24 + z * (-1.0 / 720 + z * (1.0 / 40320))))
    odd = (q & 1) == 1
    cc = jnp.where(odd, s, c)
    ss = jnp.where(odd, c, s)
    return (
        jnp.where(((q + 1) & 2) != 0, -cc, cc),
        jnp.where((q & 2) != 0, -ss, ss),
    )


def split(x):
    hi = x.astype(BF16)
    return hi, (x - hi.astype(F32)).astype(BF16)


def dot(a, b):
    return lax.dot_general(a, b, (((1,), (0,)), ((), ())), preferred_element_type=F32)


def dot_t(a, b):
    return lax.dot_general(a, b, (((1,), (1,)), ((), ())), preferred_element_type=F32)


def dot3(a, b):
    ah, al = split(a)
    bh, bl = split(b)
    return dot(ah, bh) + (dot(ah, bl) + dot(al, bh))


def kernel(
    cs_ref, ss_ref, vc_ref, vr_ref, vw_ref, fac_hbm,
    cor_hbm, img_hbm,
    xv, rhi, rlo, tabh, tabl, phase, part, rec_k, snd_y, rec_y,
    snd_a, rec_a, d1, twc, tws, gai_s, gai_r, g_s, g_r,
    snd_b, rec_b, agb, cor_v, img_v,
    load_sem, out_sem, ks_sem, kr_sem, ys_sem, yr_sem,
    gs_sem, gr_sem, as_sem, ar_sem, cs_sem, cr_sem, bs_sem, br_sem,
    ags_sem, agr_sem, fws_sem, fwr_sem,
):
    r = lax.axis_index("frow")
    c = lax.axis_index("fcol")
    y = c // 4
    h = (c // 2) % 2
    k = c % 2
    low_y = 1 - y // 2
    dev_k = (r, c + 1 - 2 * k)
    y_of = [y, 3 - y, (y + 2) % 4, (5 - y) % 4]
    h_of = [h, 1 - h]
    near = [(0, 1), (1, 0), (1, 1)]
    far = [(2, 0), (3, 0), (2, 1), (3, 1)]
    rels = near + far

    def dev_yh(rel):
        return (r, y_of[rel[0]] * 4 + h_of[rel[1]] * 2 + k)

    def group(rel):
        return rel[0] // 2

    r_peers = [(r + d) % NR for d in range(NR)]
    dev_r = [(rp, c) for rp in r_peers]

    def remote(src, dst, ssem, rsem, dev):
        return pltpu.make_async_remote_copy(
            src_ref=src, dst_ref=dst, send_sem=ssem, recv_sem=rsem,
            device_id=dev, device_id_type=MESH,
        )

    barrier = pltpu.get_barrier_semaphore()
    for dev in [dev_k] + [dev_yh(rel) for rel in rels] + dev_r[1:]:
        pl.semaphore_signal(barrier, inc=1, device_id=dev, device_id_type=MESH)

    load = pltpu.make_async_copy(fac_hbm, xv, load_sem)
    load.start()

    f = cs_ref[0]
    off = c * LW
    pair = (y + 1) // 2 % 2
    base_of = [128 * (1 - pair), 128 * pair]
    coord = off + iota((16, LW), 1)
    u = iota((16, LW), 0)
    ibase = jnp.where(u < 8, base_of[0], base_of[1]) + (u & 7) * 16
    ac, asn = sincos(((2 * ibase + 1) * coord) & (2 * N2 - 1), 15)
    bc, bs = sincos((2 * u * coord) & (2 * N2 - 1), 15)
    pc, ps = sincos(((2 * f + SG - 1) * (off + iota((8, LW), 1))) & (2 * N2 - 1), 15)
    pc = pc[0:1] * F32(1.0 / math.sqrt(N2))
    ps = ps[0:1] * F32(1.0 / math.sqrt(N2))
    phase[0:1, :] = pc
    phase[1:2, :] = ps

    def table_group(g):
        for n in range(8):
            ca = ac[g * 8 + n : g * 8 + n + 1]
            sa = asn[g * 8 + n : g * 8 + n + 1]
            th, tl = split(ca * bc - sa * bs)
            tabh[g, n * 16 : n * 16 + 16, :] = th
            tabl[g, n * 16 : n * 16 + 16, :] = tl
            th, tl = split(sa * bc + ca * bs)
            tabh[g, 128 + n * 16 : 144 + n * 16, :] = th
            tabl[g, 128 + n * 16 : 144 + n * 16, :] = tl

    table_group(1)
    load.wait()
    xr = xv[0]
    xi = xv[1]
    hi, lo = split(xr * pc + xi * ps)
    rhi[0:LH] = hi
    rlo[0:LH] = lo
    hi, lo = split(xi * pc - xr * ps)
    rhi[LH:] = hi
    rlo[LH:] = lo

    def strip_group(g):
        a = tabh[g]
        acc = dot_t(a, rhi[...]) + (dot_t(a, rlo[...]) + dot_t(tabl[g], rhi[...]))
        for hh in range(2):
            for kk in range(2):
                base = (hh * 2 + kk) * 32
                ar = acc[base : base + 32, :LH]
                ai = acc[base : base + 32, LH:]
                br = acc[128 + base : 160 + base, :LH]
                bi = acc[128 + base : 160 + base, LH:]
                part[g, kk, 0, hh, 0] = ar + bi
                part[g, kk, 0, hh, 1] = ai - br
                part[g, 1 - kk, 1, 1 - hh, 0] = ar - bi
                part[g, 1 - kk, 1, 1 - hh, 1] = ai + br

    strip_group(1)
    table_group(0)
    pl.semaphore_wait(barrier, 23)
    k_copies = [
        remote(part.at[g, 1 - k], rec_k.at[g], ks_sem.at[g], kr_sem.at[g], dev_k) for g in range(2)
    ]
    k_copies[1].start()
    strip_group(0)
    k_copies[0].start()

    def send_group(g, group_rels):
        k_copies[g].wait_recv()
        for sg in range(2):
            for hh in range(2):
                snd_y[g, sg, hh] = part[g, k, sg, hh] + rec_k[g, sg, hh]
        copies = [
            remote(
                snd_y.at[g, 1 - y_of[rel[0]] // 2, h_of[rel[1]]],
                rec_y.at[rels.index(rel)], ys_sem.at[g], yr_sem.at[g], dev_yh(rel),
            )
            for rel in group_rels
        ]
        for cp in copies:
            cp.start()

    send_group(1, far)
    send_group(0, near)

    rows_l = vr_ref[...]
    diag = iota((MAXB, MAXB), 0) == iota((MAXB, MAXB), 1)
    row_c = jnp.sum(
        jnp.where(diag, jnp.broadcast_to(rows_l, (MAXB, MAXB)).astype(F32), 0.0), axis=1, keepdims=True
    )
    row_c = row_c.astype(I32)
    wide = NR * 128
    lane = iota((32, wide), 1)
    place = ((lane >> 6) & 1) * 16 + (lane >> 7)
    place = place + low_y * (31 - 2 * place)
    sel = (iota((32, wide), 0) == place).astype(F32).astype(BF16)
    w = vw_ref[0].T
    w1 = w.astype(BF16)
    rest = w - w1.astype(F32)
    w2 = rest.astype(BF16)
    w3 = (rest - w2.astype(F32)).astype(BF16)
    wide_w = (dot(w1, sel) + dot(w2, sel)) + dot(w3, sel)
    wide_w = jnp.where((row_c >> 4) == (iota((MAXB, wide), 1) & 31), wide_w, 0.0)
    wh, wl = split(wide_w)
    low = jnp.broadcast_to(rows_l, (16, MAXB)) & 15
    lhs = ((low == iota((16, MAXB), 0)) & (iota((16, MAXB), 1) < vc_ref[0])).astype(F32).astype(BF16)
    gain = 1.0 + (dot(lhs, wh) + dot(lhs, wl))
    for i in range(NR):
        gai_s[i] = gain[:, i * 128 : (i + 1) * 128]

    def exchange(src, dst, slot, ssem, rsem):
        for d in range(1, NR):
            remote(src.at[r_peers[d]], dst.at[slot], ssem, rsem, dev_r[d]).start()

    def all_of(dst, ssem, rsem):
        some = dst.at[pl.ds(0, NR - 1)]
        return remote(some, some, ssem, rsem, dev_r[1])

    exchange(gai_s, gai_r, r, gs_sem, gr_sem)
    gai_r[r] = gai_s[r]

    mu = iota((16, 128), 0)
    lb = iota((16, 128), 1)

    @pl.loop(0, NR)
    def _(s):
        kf = (ss_ref[s] + mu) & (N1 - 1)
        rows = pl.ds(pl.multiple_of(s * 16, 16), 16)
        cc, sn = sincos((kf * lb) & (N1 - 1), 11)
        twc[rows, :] = cc * F32(1.0 / math.sqrt(N1))
        tws[rows, :] = sn * F32(1.0 / math.sqrt(N1))
        ca, sa = sincos((kf * (lb & 15)) & 15, 4)
        pi = (lb >> 4) & 1
        blk = lb >> 5
        for po in range(2):
            v = jnp.where(pi == 0, ca, sa) if po == 0 else jnp.where(pi == 0, -sa, ca)
            hi = v.astype(BF16).astype(F32)
            v = jnp.where(blk < 2, hi, jnp.where(blk == 2, v - hi, 0.0))
            d1[po, rows, :] = v.astype(BF16)

    row = iota((512, 128), 0)
    col = iota((512, 128), 1)
    cc, sn = sincos(((row & 127) * (col & 31)) & 127, 7)
    pin = (row >> 7) & 1
    pout = (col >> 5) & 1
    same = (row >> 8) == (col >> 6)
    e3 = jnp.where(pin == pout, cc, jnp.where(pin == 1, sn, -sn))
    e3h, e3l = split(jnp.where(same, e3, 0.0))
    row = iota((128, 512), 0)
    col = iota((128, 512), 1)
    cc, sn = sincos(((col & 127) * (row & 31)) & 127, 7)
    pin = (row >> 5) & 1
    pout = (col >> 7) & 1
    same = (col >> 8) == (row >> 6)
    e4 = jnp.where(pin == pout, cc, jnp.where(pin == 1, -sn, sn))
    e4h, e4l = split(jnp.where(same, e4, 0.0))
    lane = iota((16, 256), 1)
    first = jnp.zeros((16, 256), I32)
    for s in range(NR):
        first = jnp.where((lane >> 4) == s, ss_ref[s], first)
    ca, sa = sincos(((first + (lane & 15)) * iota((16, 256), 0)) & 15, 4)
    d2 = jnp.concatenate(
        [jnp.concatenate([ca, -sa], axis=1), jnp.concatenate([sa, ca], axis=1)], axis=0
    )
    d2h, d2l = split(d2)

    far_in = rec_y.at[pl.ds(3, 4)]
    near_in = rec_y.at[pl.ds(0, 3)]
    far_all = remote(far_in, far_in, ys_sem.at[1], yr_sem.at[1], dev_yh(far[0]))
    near_all = remote(near_in, near_in, ys_sem.at[0], yr_sem.at[0], dev_yh(near[0]))
    near_all.wait_recv()
    far_all.wait_recv()
    strip = (
        (snd_y[0, low_y, h] + rec_y[0]) + (rec_y[1] + rec_y[2])
    ) + ((rec_y[3] + rec_y[4]) + (rec_y[5] + rec_y[6]))
    for p in range(2):
        for q in range(2):
            snd_a[:, p * 2 + q, :] = strip[p, q * 16 : (q + 1) * 16, :]
    exchange(snd_a, rec_a, r, as_sem, ar_sem)
    rec_a[r] = snd_a[r]
    all_of(gai_r, gs_sem, gr_sem).wait_recv()
    all_of(rec_a, as_sem, ar_sem).wait_recv()

    v = jnp.concatenate(
        [jnp.concatenate([rec_a[:, p * 2 + q, :] for q in range(2)], axis=1) for p in range(2)], axis=0
    )
    vh, vl = split(v)
    stack = jnp.concatenate([vh, vl, vh, jnp.zeros_like(vh)], axis=0)
    zre = dot(d1[0], stack)
    zim = dot(d1[1], stack)
    tc = twc[...]
    ts = tws[...]
    cols = []
    for q in range(2):
        re = zre[:, q * 128 : (q + 1) * 128]
        im = zim[:, q * 128 : (q + 1) * 128]
        cols += [re * tc + im * ts, im * tc - re * ts]
    zh, zl = split(jnp.concatenate(cols, axis=1))
    sub = dot(zh, e3h) + (dot(zh, e3l) + dot(zl, e3h))
    grid = sub * gai_r[...].reshape(256, 128)
    g_s[...] = grid.reshape(NR, 16, 128)
    gh, gl = split(grid)
    vv = dot(gh, e4h) + (dot(gh, e4l) + dot(gl, e4h))
    res = []
    ims = []
    for q in range(2):
        re = vv[:, q * 256 : q * 256 + 128]
        im = vv[:, q * 256 + 128 : q * 256 + 256]
        res.append(re * tc - im * ts)
        ims.append(im * tc + re * ts)
    both = jnp.concatenate([jnp.concatenate(res, axis=1), jnp.concatenate(ims, axis=1)], axis=0)
    bh, bl = split(both)
    back = dot(d2h, bh) + (dot(d2h, bl) + dot(d2l, bh))
    for p in range(2):
        for q in range(2):
            snd_b[:, p * 2 + q, :] = back[p * 16 : (p + 1) * 16, q * 128 : (q + 1) * 128]
    exchange(snd_b, rec_b, r, bs_sem, br_sem)
    slot = r + low_y * (NR - 1 - 2 * r)
    exchange(g_s, g_r, slot, cs_sem, cr_sem)
    rec_b[r] = snd_b[r]
    g_r[slot] = g_s[r]
    all_of(rec_b, bs_sem, br_sem).wait_recv()
    for p in range(2):
        for q in range(2):
            agb[0, k, low_y, h, p, q * 16 : (q + 1) * 16, :] = rec_b[:, p * 2 + q, :]

    mine = agb.at[0, k, low_y, h]
    sends = [
        remote(mine, agb.at[group(rel), k, low_y, h], ags_sem.at[i], agr_sem.at[i], dev_yh(rel))
        for i, rel in enumerate(rels)
    ]
    for cp in sends[3:] + sends[:3]:
        cp.start()

    def block(rel, kk):
        return agb.at[group(rel), kk, 1 - y_of[rel[0]] // 2, h_of[rel[1]]]

    forwards = [
        remote(block(rel, k), block(rel, k), fws_sem.at[i], fwr_sem.at[i], dev_k)
        for i, rel in enumerate(rels + [(0, 0)])
    ]
    forwards[7].start()

    def arrive(i):
        ref = block(rels[i], k)
        remote(ref, ref, ags_sem.at[i], agr_sem.at[i], dev_yh(rels[i])).wait_recv()
        forwards[i].start()

    def forwarded(i):
        ref = block((rels + [(0, 0)])[i], 1 - k)
        remote(ref, ref, fws_sem.at[i], fwr_sem.at[i], dev_k).wait_recv()

    for i in range(7):
        arrive(i)

    def image_lhs(g):
        er, ei, om, orr = [], [], [], []
        for hh in range(2):
            for kk in range(2):
                up = agb[g, kk, 0, hh]
                dn = agb[g, 1 - kk, 1, 1 - hh]
                er.append(up[0] + dn[0])
                ei.append(up[1] + dn[1])
                om.append(dn[1] - up[1])
                orr.append(up[0] - dn[0])
        t = [jnp.concatenate(x, axis=0).T for x in (er, om, ei, orr)]
        return split(
            jnp.concatenate(
                [jnp.concatenate(t[:2], axis=1), jnp.concatenate(t[2:], axis=1)], axis=0
            )
        )

    for i in (7, 0, 1, 2):
        forwarded(i)
    lh, ll = image_lhs(0)
    for n in range(4):
        cols = slice(n * 256, (n + 1) * 256)
        o = dot(lh, tabh[0, :, cols]) + (dot(ll, tabh[0, :, cols]) + dot(lh, tabl[0, :, cols]))
        img_v[0, :, cols] = o[:LH]
        img_v[1, :, cols] = o[LH:]
    for i in (3, 4, 5, 6):
        forwarded(i)
    lh, ll = image_lhs(1)
    outs = []
    for n in range(4):
        cols = slice(n * 256, (n + 1) * 256)
        o = dot(lh, tabh[1, :, cols]) + (dot(ll, tabh[1, :, cols]) + dot(lh, tabl[1, :, cols]))
        re = img_v[0, :, cols] + o[:LH]
        im = img_v[1, :, cols] + o[LH:]
        pc = phase[0:1, cols]
        ps = phase[1:2, cols]
        img_v[0, :, cols] = re * pc - im * ps
        img_v[1, :, cols] = im * pc + re * ps
        cp = pltpu.make_async_copy(img_v.at[:, :, cols], img_hbm.at[:, :, cols], out_sem.at[n])
        cp.start()
        outs.append(cp)

    all_of(g_r, cs_sem, cr_sem).wait_recv()
    lane = iota((128, SG), 1)
    rowi = iota((128, SG), 0)
    gath = g_r[...].reshape(256, 128)
    g1 = gath.astype(BF16)
    rest = gath - g1.astype(F32)
    g2 = rest.astype(BF16)
    g3 = (rest - g2.astype(F32)).astype(BF16)
    keep = (iota((256, SG), 0) & 15) == (iota((256, SG), 1) & 15)
    for q in range(2):
        qq = q + low_y * (1 - 2 * q)
        for p in range(2):
            ex = (rowi == (q * 2 + p) * 32 + (lane >> 4)).astype(F32).astype(BF16)
            wide_g = (dot(g1, ex) + dot(g2, ex)) + dot(g3, ex)
            wide_g = jnp.where(keep, wide_g, 0.0)
            cor_v[0, pl.ds(qq * 16, 16), p, :] = jnp.sum(wide_g.reshape(16, 16, SG), axis=1)
    cor_out = pltpu.make_async_copy(cor_v, cor_hbm, out_sem.at[4])
    cor_out.start()

    for cp in k_copies + sends + forwards:
        cp.wait_send()
    far_all.wait_send()
    near_all.wait_send()
    all_of(gai_r, gs_sem, gr_sem).wait_send()
    all_of(rec_a, as_sem, ar_sem).wait_send()
    all_of(g_r, cs_sem, cr_sem).wait_send()
    all_of(rec_b, bs_sem, br_sem).wait_send()
    for cp in outs:
        cp.wait()
    cor_out.wait()


def per_device(facets, column_start, subgrid_start, vis_count, vis_row, vis_weight):
    dma = pltpu.SemaphoreType.DMA
    vm = pltpu.VMEM
    smem = pl.BlockSpec(memory_space=pltpu.SMEM)
    vmem = pl.BlockSpec(memory_space=pltpu.VMEM)
    anym = pl.BlockSpec(memory_space=pl.ANY)
    return pl.pallas_call(
        kernel,
        out_shape=(
            jax.ShapeDtypeStruct((1, 32, 2, SG), F32),
            jax.ShapeDtypeStruct((2, LH, LW), F32),
        ),
        in_specs=[smem, smem, smem, vmem, vmem, anym],
        out_specs=(anym, anym),
        scratch_shapes=[
            vm((2, LH, LW), F32),
            vm((2 * LH, LW), BF16),
            vm((2 * LH, LW), BF16),
            vm((2, 256, LW), BF16),
            vm((2, 256, LW), BF16),
            vm((8, LW), F32),
            vm((2, 2, 2, 2, 2, 32, LH), F32),
            vm((2, 2, 2, 2, 32, LH), F32),
            vm((2, 2, 2, 2, 32, LH), F32),
            vm((7, 2, 32, LH), F32),
            vm((NR, 4, 128), F32),
            vm((NR, 4, 128), F32),
            vm((2, 256, 128), BF16),
            vm((256, 128), F32),
            vm((256, 128), F32),
            vm((NR, 16, 128), F32),
            vm((NR, 16, 128), F32),
            vm((NR, 16, 128), F32),
            vm((NR, 16, 128), F32),
            vm((NR, 4, 128), F32),
            vm((NR, 4, 128), F32),
            vm((2, 2, 2, 2, 2, 32, LH), F32),
            vm((1, 32, 2, SG), F32),
            vm((2, LH, LW), F32),
            dma, dma((5,)), dma((2,)), dma((2,)), dma((2,)), dma((2,)),
            dma, dma, dma, dma, dma, dma, dma, dma,
            dma((7,)), dma((7,)), dma((8,)), dma((8,)),
        ],
        compiler_params=pltpu.CompilerParams(collective_id=0, has_side_effects=True),
    )(column_start, subgrid_start, vis_count, vis_row, jnp.transpose(vis_weight, (0, 2, 1)), facets)


def solution(mesh):
    return jax.shard_map(
        per_device,
        mesh=mesh,
        in_specs=(
            P(None, "frow", "fcol"),
            P(),
            P(),
            P("frow"),
            P("frow", None),
            P("frow", None, "fcol"),
        ),
        out_specs=(P("frow", "fcol", None, None), P(None, "frow", "fcol")),
        check_vma=False,
    )
```

time: 56.6 us -> 48 us (0.85)
  Pallas kernels: 49.1 us -> 41.9 us
  local copies, waits for them, and re-layouts: 5.29 us -> 3.87 us
    pallas_call x1, Pallas kernels: 49.1 us -> 41.9 us  [per_device(): pl.pallas_call(kernel, out_shape=(jax.ShapeDtypeStruct((1, 32, 2, SG), F3...]
    unnamed x3 -> x2, local copies, waits for them, and re-layouts: 5.29 us -> 3.87 us
where the time goes in v2:
time: 48 us; the launch traced here: 47.7 us
  Pallas kernels  41.9 us (87%)
  local copies, waits for them, and re-layouts  3.87 us (8%)
  between operations  1.93 us (4%)
    pallas_call x1, Pallas kernels, per_device(): pl.pallas_call(kernel, out_shape=(jax.ShapeDtypeStruct((1, 32, 2, SG), F3...  41.9 us
    unnamed x2, local copies, waits for them, and re-layouts  3.87 us

profile of v2, /device:TPU:1, one launch (start us, length us, event | category | flops | bytes accessed | tf_op | source)
XLA Modules:
  0.0 47.7 jit_solution(16014506632372022712)
XLA Ops:
  1.9 41.9 %shard_map.77 = (f32[1,32,2,512]{3,2,1,0:T(2,128)}, f32[2,128,1024]{2,1,0:T(8,128)}) custom-call(s32[1]{0:T(128)S(6)} %copy.10.cs_ref, s32[16]{0:T(128)} %ss_ref.1, s32[1]{0:T(128)S(6)} %copy.11.vc_ref, s32[1,64]{1,0:T(1,128)} %vr_ref.1, f32[1,32,64]{2,1,0:T(8,128)} %bitcast.1, f32[2,128,1024]{2,1,0:T(8,128)} %fac_hbm.1), custom_call_target="tpu_custom_call" | custom-call | tf_op jit(solution)/shard_map/pallas_call | solution.py:439
  43.8 1.6 %copy.12 = f32[1,32,2,512]{3,2,1,0:T(2,128)} copy(f32[1,32,2,512]{3,2,1,0:T(2,128)} %get-tuple-element.4) | data formatting | bytes 262144
  45.4 2.3 %copy.13 = f32[2,128,1024]{2,1,0:T(8,128)} copy(f32[2,128,1024]{2,1,0:T(8,128)} %get-tuple-element.5) | data formatting | bytes 2097152

commit v3 on v2

--- a/solution.py
+++ b/solution.py
@@ -62,8 +62,9 @@
 
 
 def kernel(
-    cs_ref, ss_ref, vc_ref, vr_ref, vw_ref, fac_hbm,
+    cs_ref, vc_ref, ss_hbm, vr_hbm, vw_hbm, fac_hbm,
     cor_hbm, img_hbm,
+    ss_ref, vr_ref, vw_ref,
     xv, rhi, rlo, tabh, tabl, phase, part, rec_k, snd_y, rec_y,
     snd_a, rec_a, d1, twc, tws, gai_s, gai_r, g_s, g_r,
     snd_b, rec_b, agb, cor_v, img_v,
@@ -80,8 +81,8 @@
     dev_k = (r, c + 1 - 2 * k)
     y_of = [y, 3 - y, (y + 2) % 4, (5 - y) % 4]
     h_of = [h, 1 - h]
-    near = [(0, 1), (1, 0), (1, 1)]
-    far = [(2, 0), (3, 0), (2, 1), (3, 1)]
+    near = [(1, 1), (0, 1), (1, 0)]
+    far = [(2, 1), (3, 1), (2, 0), (3, 0)]
     rels = near + far
 
     def dev_yh(rel):
@@ -99,12 +100,18 @@
             device_id=dev, device_id_type=MESH,
         )
 
+    load = pltpu.make_async_copy(fac_hbm, xv, load_sem.at[0])
+    load.start()
+    small = [
+        pltpu.make_async_copy(a, b, load_sem.at[i + 1])
+        for i, (a, b) in enumerate([(vr_hbm, vr_ref), (vw_hbm, vw_ref), (ss_hbm, ss_ref)])
+    ]
+    for cp in small:
+        cp.start()
+
     barrier = pltpu.get_barrier_semaphore()
     for dev in [dev_k] + [dev_yh(rel) for rel in rels] + dev_r[1:]:
         pl.semaphore_signal(barrier, inc=1, device_id=dev, device_id_type=MESH)
-
-    load = pltpu.make_async_copy(fac_hbm, xv, load_sem)
-    load.start()
 
     f = cs_ref[0]
     off = c * LW
@@ -186,6 +193,8 @@
     send_group(1, far)
     send_group(0, near)
 
+    for cp in small:
+        cp.wait()
     rows_l = vr_ref[...]
     diag = iota((MAXB, MAXB), 0) == iota((MAXB, MAXB), 1)
     row_c = jnp.sum(
@@ -353,6 +362,20 @@
         ref = block((rels + [(0, 0)])[i], 1 - k)
         remote(ref, ref, fws_sem.at[i], fwr_sem.at[i], dev_k).wait_recv()
 
+    all_of(g_r, cs_sem, cr_sem).wait_recv()
+    lane = iota((256, SG), 1)
+    rowi = iota((256, SG), 0)
+    gath = jnp.concatenate(split(g_r[...].reshape(256, 128)), axis=1)
+    keep = (rowi & 15) == (lane & 15)
+    for q in range(2):
+        qq = q + low_y * (1 - 2 * q)
+        for p in range(2):
+            ex = ((rowi & 127) == (q * 2 + p) * 32 + (lane >> 4)).astype(F32).astype(BF16)
+            wide_g = jnp.where(keep, dot(gath, ex), 0.0)
+            cor_v[0, pl.ds(qq * 16, 16), p, :] = jnp.sum(wide_g.reshape(16, 16, SG), axis=1)
+    cor_out = pltpu.make_async_copy(cor_v, cor_hbm, out_sem.at[4])
+    cor_out.start()
+
     for i in range(7):
         arrive(i)
 
@@ -398,25 +421,6 @@
         cp.start()
         outs.append(cp)
 
-    all_of(g_r, cs_sem, cr_sem).wait_recv()
-    lane = iota((128, SG), 1)
-    rowi = iota((128, SG), 0)
-    gath = g_r[...].reshape(256, 128)
-    g1 = gath.astype(BF16)
-    rest = gath - g1.astype(F32)
-    g2 = rest.astype(BF16)
-    g3 = (rest - g2.astype(F32)).astype(BF16)
-    keep = (iota((256, SG), 0) & 15) == (iota((256, SG), 1) & 15)
-    for q in range(2):
-        qq = q + low_y * (1 - 2 * q)
-        for p in range(2):
-            ex = (rowi == (q * 2 + p) * 32 + (lane >> 4)).astype(F32).astype(BF16)
-            wide_g = (dot(g1, ex) + dot(g2, ex)) + dot(g3, ex)
-            wide_g = jnp.where(keep, wide_g, 0.0)
-            cor_v[0, pl.ds(qq * 16, 16), p, :] = jnp.sum(wide_g.reshape(16, 16, SG), axis=1)
-    cor_out = pltpu.make_async_copy(cor_v, cor_hbm, out_sem.at[4])
-    cor_out.start()
-
     for cp in k_copies + sends + forwards:
         cp.wait_send()
     far_all.wait_send()
@@ -430,21 +434,39 @@
     cor_out.wait()
 
 
+def emit(cor_in, img_in, cor_out, img_out, sem):
+    copies = [
+        pltpu.make_async_copy(img_in, img_out, sem.at[0]),
+        pltpu.make_async_copy(cor_in, cor_out, sem.at[1]),
+    ]
+    for cp in copies:
+        cp.start()
+    for cp in copies:
+        cp.wait()
+
+
 def per_device(facets, column_start, subgrid_start, vis_count, vis_row, vis_weight):
     dma = pltpu.SemaphoreType.DMA
     vm = pltpu.VMEM
     smem = pl.BlockSpec(memory_space=pltpu.SMEM)
-    vmem = pl.BlockSpec(memory_space=pltpu.VMEM)
+    hbm = pl.BlockSpec(memory_space=pltpu.HBM)
     anym = pl.BlockSpec(memory_space=pl.ANY)
-    return pl.pallas_call(
+    stay = [
+        pltpu.with_memory_space_constraint(x, pltpu.HBM)
+        for x in (subgrid_start, vis_row, jnp.transpose(vis_weight, (0, 2, 1)), facets)
+    ]
+    cor, img = pl.pallas_call(
         kernel,
         out_shape=(
             jax.ShapeDtypeStruct((1, 32, 2, SG), F32),
             jax.ShapeDtypeStruct((2, LH, LW), F32),
         ),
-        in_specs=[smem, smem, smem, vmem, vmem, anym],
+        in_specs=[smem, smem, hbm, hbm, hbm, hbm],
         out_specs=(anym, anym),
         scratch_shapes=[
+            pltpu.SMEM((NR,), I32),
+            vm((1, MAXB), I32),
+            vm((1, 32, MAXB), F32),
             vm((2, LH, LW), F32),
             vm((2 * LH, LW), BF16),
             vm((2 * LH, LW), BF16),
@@ -469,12 +491,23 @@
             vm((2, 2, 2, 2, 2, 32, LH), F32),
             vm((1, 32, 2, SG), F32),
             vm((2, LH, LW), F32),
-            dma, dma((5,)), dma((2,)), dma((2,)), dma((2,)), dma((2,)),
+            dma((4,)), dma((5,)), dma((2,)), dma((2,)), dma((2,)), dma((2,)),
             dma, dma, dma, dma, dma, dma, dma, dma,
             dma((7,)), dma((7,)), dma((8,)), dma((8,)),
         ],
-        compiler_params=pltpu.CompilerParams(collective_id=0, has_side_effects=True),
-    )(column_start, subgrid_start, vis_count, vis_row, jnp.transpose(vis_weight, (0, 2, 1)), facets)
+        compiler_params=pltpu.CompilerParams(collective_id=0, has_side_effects=True, vmem_limit_bytes=16 * 1024 * 1024),
+    )(column_start, vis_count, *stay)
+    return pl.pallas_call(
+        emit,
+        out_shape=(
+            jax.ShapeDtypeStruct((1, 32, 2, SG), F32),
+            jax.ShapeDtypeStruct((2, LH, LW), F32),
+        ),
+        in_specs=[anym, anym],
+        out_specs=(hbm, hbm),
+        scratch_shapes=[dma((2,))],
+        compiler_params=pltpu.CompilerParams(vmem_limit_bytes=4 * 1024 * 1024),
+    )(cor, img)
 
 
 def solution(mesh):

time: 48 us -> 42.7 us (0.89)
  local copies, waits for them, and re-layouts: 3.87 us -> 0 us
  Pallas kernels: 41.9 us -> 40.6 us
    unnamed x2 -> x0, local copies, waits for them, and re-layouts: 3.87 us -> none
    pallas_call x1, Pallas kernels: 41.9 us -> 39.6 us  [per_device(): pl.pallas_call(kernel, out_shape=(jax.ShapeDtypeStruct((1, 32, 2, SG), F3...]
    pallas_call x0 -> x1, Pallas kernels: none -> 1.02 us  [per_device(): pl.pallas_call(emit, out_shape=(jax.ShapeDtypeStruct((1, 32, 2, SG), F32)...]
where the time goes in v3:
time: 42.7 us; the launch traced here: 42.5 us
  Pallas kernels  40.6 us (95%)
  between operations  1.93 us (5%)
    pallas_call x1, Pallas kernels, per_device(): pl.pallas_call(kernel, out_shape=(jax.ShapeDtypeStruct((1, 32, 2, SG), F3...  39.6 us
    pallas_call x1, Pallas kernels, per_device(): pl.pallas_call(emit, out_shape=(jax.ShapeDtypeStruct((1, 32, 2, SG), F32)...  1.02 us

profile of v3, /device:TPU:1, one launch (start us, length us, event | category | flops | bytes accessed | tf_op | source)
XLA Modules:
  0.0 42.5 jit_solution(16598718695963154332)
XLA Ops:
  1.9 39.6 %shard_map.77 = (f32[1,32,2,512]{3,2,1,0:T(2,128)S(1)}, f32[2,128,1024]{2,1,0:T(8,128)S(1)}) custom-call(s32[1]{0:T(128)S(6)} %copy.8.cs_ref, s32[1]{0:T(128)S(6)} %copy.9.vc_ref, s32[16]{0:T(128)} %ss_hbm.1, s32[1,64]{1,0:T(1,128)} %vr_hbm.1, f32[1,32,64]{2,1,0:T(8,128)} %bitcast.1, f32[2,128,1024]{2,1,0:T(8,128)} %fac_hbm.1), custom_call_target="tpu_custom_call" | custom-call | tf_op jit(solution)/shard_map/pallas_call | solution.py:458
  41.5 1.0 %shard_map.78 = (f32[1,32,2,512]{3,2,1,0:T(2,128)}, f32[2,128,1024]{2,1,0:T(8,128)}) custom-call(f32[1,32,2,512]{3,2,1,0:T(2,128)S(1)} %get-tuple-element.4.cor_in, f32[2,128,1024]{2,1,0:T(8,128)S(1)} %get-tuple-element.5.img_in), custom_call_target="tpu_custom_call" | custom-call | tf_op jit(solution)/shard_map/pallas_call | solution.py:500

commit v4 on v3

--- a/solution.py
+++ b/solution.py
@@ -55,20 +55,21 @@
     return lax.dot_general(a, b, (((1,), (1,)), ((), ())), preferred_element_type=F32)
 
 
-def dot3(a, b):
+def dot3(a, bh, bl):
+    n = a.shape[0]
     ah, al = split(a)
-    bh, bl = split(b)
-    return dot(ah, bh) + (dot(ah, bl) + dot(al, bh))
+    both = dot(jnp.concatenate([ah, al], axis=0), bh)
+    return both[:n] + (dot(ah, bl) + both[n:])
 
 
 def kernel(
     cs_ref, vc_ref, ss_hbm, vr_hbm, vw_hbm, fac_hbm,
-    cor_hbm, img_hbm,
+    cor_v, img_v, lhs_v, farh, farl, phase,
     ss_ref, vr_ref, vw_ref,
-    xv, rhi, rlo, tabh, tabl, phase, part, rec_k, snd_y, rec_y,
+    xv, tabh, tabl, part, rec_k, snd_y, rec_y,
     snd_a, rec_a, d1, twc, tws, gai_s, gai_r, g_s, g_r,
-    snd_b, rec_b, agb, cor_v, img_v,
-    load_sem, out_sem, ks_sem, kr_sem, ys_sem, yr_sem,
+    snd_b, rec_b, agb,
+    load_sem, ks_sem, kr_sem, ys_sem, yr_sem,
     gs_sem, gr_sem, as_sem, ar_sem, cs_sem, cr_sem, bs_sem, br_sem,
     ags_sem, agr_sem, fws_sem, fwr_sem,
 ):
@@ -93,6 +94,7 @@
 
     r_peers = [(r + d) % NR for d in range(NR)]
     dev_r = [(rp, c) for rp in r_peers]
+    by_distance = sorted(range(1, NR), key=lambda d: abs(d - NR // 2))
 
     def remote(src, dst, ssem, rsem, dev):
         return pltpu.make_async_remote_copy(
@@ -110,49 +112,67 @@
         cp.start()
 
     barrier = pltpu.get_barrier_semaphore()
-    for dev in [dev_k] + [dev_yh(rel) for rel in rels] + dev_r[1:]:
+    for dev in [dev_r[d] for d in by_distance] + [dev_yh(rel) for rel in far + near] + [dev_k]:
         pl.semaphore_signal(barrier, inc=1, device_id=dev, device_id_type=MESH)
 
     f = cs_ref[0]
     off = c * LW
     pair = (y + 1) // 2 % 2
     base_of = [128 * (1 - pair), 128 * pair]
-    coord = off + iota((16, LW), 1)
-    u = iota((16, LW), 0)
+    u = iota((16, 128), 0)
+    place = off + iota((16, 128), 1)
     ibase = jnp.where(u < 8, base_of[0], base_of[1]) + (u & 7) * 16
-    ac, asn = sincos(((2 * ibase + 1) * coord) & (2 * N2 - 1), 15)
-    bc, bs = sincos((2 * u * coord) & (2 * N2 - 1), 15)
-    pc, ps = sincos(((2 * f + SG - 1) * (off + iota((8, LW), 1))) & (2 * N2 - 1), 15)
-    pc = pc[0:1] * F32(1.0 / math.sqrt(N2))
-    ps = ps[0:1] * F32(1.0 / math.sqrt(N2))
-    phase[0:1, :] = pc
-    phase[1:2, :] = ps
-
-    def table_group(g):
+    turns = [2 * ibase + 1, 2 * u, jnp.full((16, 128), 2 * f + SG - 1, I32)]
+    now = [sincos((n * place) & (2 * N2 - 1), 15) for n in turns]
+    step = [sincos((n * 128) & (2 * N2 - 1), 15) for n in turns]
+
+    def table_tile(g, a, b):
+        tiles = []
         for n in range(8):
-            ca = ac[g * 8 + n : g * 8 + n + 1]
-            sa = asn[g * 8 + n : g * 8 + n + 1]
-            th, tl = split(ca * bc - sa * bs)
-            tabh[g, n * 16 : n * 16 + 16, :] = th
-            tabl[g, n * 16 : n * 16 + 16, :] = tl
-            th, tl = split(sa * bc + ca * bs)
-            tabh[g, 128 + n * 16 : 144 + n * 16, :] = th
-            tabl[g, 128 + n * 16 : 144 + n * 16, :] = tl
-
-    table_group(1)
+            ca = a[0][g * 8 + n : g * 8 + n + 1]
+            sa = a[1][g * 8 + n : g * 8 + n + 1]
+            tiles.append(split(ca * b[0] - sa * b[1]) + split(sa * b[0] + ca * b[1]))
+        return [
+            jnp.concatenate([t[e] for t in tiles] + [t[e + 2] for t in tiles], axis=0)
+            for e in range(2)
+        ]
+
+    columns = [[], []]
+    waves = []
+    for n in range(8):
+        for g in range(2):
+            columns[g].append(table_tile(g, now[0], now[1]))
+        waves.append([w[0:1] * F32(1.0 / math.sqrt(N2)) for w in now[2]])
+        now = [
+            (ca * cb - sa * sb, sa * cb + ca * sb) for (ca, sa), (cb, sb) in zip(now, step)
+        ]
+    tables = [
+        [jnp.concatenate([t[e] for t in columns[g]], axis=1) for e in range(2)] for g in range(2)
+    ]
+
     load.wait()
-    xr = xv[0]
-    xi = xv[1]
-    hi, lo = split(xr * pc + xi * ps)
-    rhi[0:LH] = hi
-    rlo[0:LH] = lo
-    hi, lo = split(xi * pc - xr * ps)
-    rhi[LH:] = hi
-    rlo[LH:] = lo
+    parts = []
+    for n in range(8):
+        cols = slice(n * 128, n * 128 + 128)
+        pc, ps = waves[n]
+        phase[0:1, cols] = pc
+        phase[1:2, cols] = ps
+        tiles = [[], []]
+        for i in range(8):
+            rows = slice(i * 16, i * 16 + 16)
+            xr = xv[0, rows, cols]
+            xi = xv[1, rows, cols]
+            tiles[0].append(split(xr * pc + xi * ps))
+            tiles[1].append(split(xi * pc - xr * ps))
+        parts.append(
+            [jnp.concatenate([t[e] for t in tiles[0] + tiles[1]], axis=0) for e in range(2)]
+        )
+    rhi, rlo = [jnp.concatenate([t[e] for t in parts], axis=1) for e in range(2)]
 
     def strip_group(g):
-        a = tabh[g]
-        acc = dot_t(a, rhi[...]) + (dot_t(a, rlo[...]) + dot_t(tabl[g], rhi[...]))
+        th, tl = tables[g]
+        both = dot_t(jnp.concatenate([th, tl], axis=0), rhi)
+        acc = both[:256] + (dot_t(th, rlo) + both[256:])
         for hh in range(2):
             for kk in range(2):
                 base = (hh * 2 + kk) * 32
@@ -166,7 +186,6 @@
                 part[g, 1 - kk, 1, 1 - hh, 1] = ai + br
 
     strip_group(1)
-    table_group(0)
     pl.semaphore_wait(barrier, 23)
     k_copies = [
         remote(part.at[g, 1 - k], rec_k.at[g], ks_sem.at[g], kr_sem.at[g], dev_k) for g in range(2)
@@ -221,15 +240,17 @@
         gai_s[i] = gain[:, i * 128 : (i + 1) * 128]
 
     def exchange(src, dst, slot, ssem, rsem):
-        for d in range(1, NR):
+        for d in by_distance:
             remote(src.at[r_peers[d]], dst.at[slot], ssem, rsem, dev_r[d]).start()
 
     def all_of(dst, ssem, rsem):
         some = dst.at[pl.ds(0, NR - 1)]
         return remote(some, some, ssem, rsem, dev_r[1])
 
-    exchange(gai_s, gai_r, r, gs_sem, gr_sem)
-    gai_r[r] = gai_s[r]
+    tabh[...] = tables[0][0]
+    tabl[...] = tables[0][1]
+    farh[...] = tables[1][0]
+    farl[...] = tables[1][1]
 
     mu = iota((16, 128), 0)
     lb = iota((16, 128), 1)
@@ -249,6 +270,9 @@
             hi = v.astype(BF16).astype(F32)
             v = jnp.where(blk < 2, hi, jnp.where(blk == 2, v - hi, 0.0))
             d1[po, rows, :] = v.astype(BF16)
+
+    exchange(gai_s, gai_r, r, gs_sem, gr_sem)
+    gai_r[r] = gai_s[r]
 
     row = iota((512, 128), 0)
     col = iota((512, 128), 1)
@@ -274,7 +298,6 @@
     d2 = jnp.concatenate(
         [jnp.concatenate([ca, -sa], axis=1), jnp.concatenate([sa, ca], axis=1)], axis=0
     )
-    d2h, d2l = split(d2)
 
     far_in = rec_y.at[pl.ds(3, 4)]
     near_in = rec_y.at[pl.ds(0, 3)]
@@ -307,12 +330,10 @@
         re = zre[:, q * 128 : (q + 1) * 128]
         im = zim[:, q * 128 : (q + 1) * 128]
         cols += [re * tc + im * ts, im * tc - re * ts]
-    zh, zl = split(jnp.concatenate(cols, axis=1))
-    sub = dot(zh, e3h) + (dot(zh, e3l) + dot(zl, e3h))
+    sub = dot3(jnp.concatenate(cols, axis=1), e3h, e3l)
     grid = sub * gai_r[...].reshape(256, 128)
     g_s[...] = grid.reshape(NR, 16, 128)
-    gh, gl = split(grid)
-    vv = dot(gh, e4h) + (dot(gh, e4l) + dot(gl, e4h))
+    vv = dot3(grid, e4h, e4l)
     res = []
     ims = []
     for q in range(2):
@@ -322,7 +343,7 @@
         ims.append(im * tc + re * ts)
     both = jnp.concatenate([jnp.concatenate(res, axis=1), jnp.concatenate(ims, axis=1)], axis=0)
     bh, bl = split(both)
-    back = dot(d2h, bh) + (dot(d2h, bl) + dot(d2l, bh))
+    back = dot3(d2, bh, bl)
     for p in range(2):
         for q in range(2):
             snd_b[:, p * 2 + q, :] = back[p * 16 : (p + 1) * 16, q * 128 : (q + 1) * 128]
@@ -373,9 +394,6 @@
             ex = ((rowi & 127) == (q * 2 + p) * 32 + (lane >> 4)).astype(F32).astype(BF16)
             wide_g = jnp.where(keep, dot(gath, ex), 0.0)
             cor_v[0, pl.ds(qq * 16, 16), p, :] = jnp.sum(wide_g.reshape(16, 16, SG), axis=1)
-    cor_out = pltpu.make_async_copy(cor_v, cor_hbm, out_sem.at[4])
-    cor_out.start()
-
     for i in range(7):
         arrive(i)
 
@@ -390,36 +408,21 @@
                 om.append(dn[1] - up[1])
                 orr.append(up[0] - dn[0])
         t = [jnp.concatenate(x, axis=0).T for x in (er, om, ei, orr)]
-        return split(
-            jnp.concatenate(
-                [jnp.concatenate(t[:2], axis=1), jnp.concatenate(t[2:], axis=1)], axis=0
-            )
+        return jnp.concatenate(
+            [jnp.concatenate(t[:2], axis=1), jnp.concatenate(t[2:], axis=1)], axis=0
         )
 
     for i in (7, 0, 1, 2):
         forwarded(i)
-    lh, ll = image_lhs(0)
+    lhs_g = image_lhs(0)
     for n in range(4):
         cols = slice(n * 256, (n + 1) * 256)
-        o = dot(lh, tabh[0, :, cols]) + (dot(ll, tabh[0, :, cols]) + dot(lh, tabl[0, :, cols]))
+        o = dot3(lhs_g, tabh[:, cols], tabl[:, cols])
         img_v[0, :, cols] = o[:LH]
         img_v[1, :, cols] = o[LH:]
     for i in (3, 4, 5, 6):
         forwarded(i)
-    lh, ll = image_lhs(1)
-    outs = []
-    for n in range(4):
-        cols = slice(n * 256, (n + 1) * 256)
-        o = dot(lh, tabh[1, :, cols]) + (dot(ll, tabh[1, :, cols]) + dot(lh, tabl[1, :, cols]))
-        re = img_v[0, :, cols] + o[:LH]
-        im = img_v[1, :, cols] + o[LH:]
-        pc = phase[0:1, cols]
-        ps = phase[1:2, cols]
-        img_v[0, :, cols] = re * pc - im * ps
-        img_v[1, :, cols] = im * pc + re * ps
-        cp = pltpu.make_async_copy(img_v.at[:, :, cols], img_hbm.at[:, :, cols], out_sem.at[n])
-        cp.start()
-        outs.append(cp)
+    lhs_v[...] = image_lhs(1)
 
     for cp in k_copies + sends + forwards:
         cp.wait_send()
@@ -429,18 +432,24 @@
     all_of(rec_a, as_sem, ar_sem).wait_send()
     all_of(g_r, cs_sem, cr_sem).wait_send()
     all_of(rec_b, bs_sem, br_sem).wait_send()
-    for cp in outs:
-        cp.wait()
-    cor_out.wait()
-
-
-def emit(cor_in, img_in, cor_out, img_out, sem):
-    copies = [
-        pltpu.make_async_copy(img_in, img_out, sem.at[0]),
-        pltpu.make_async_copy(cor_in, cor_out, sem.at[1]),
-    ]
-    for cp in copies:
+
+
+def emit(cor_v, img_v, lhs_v, farh, farl, phase, cor_hbm, img_hbm, buf, sem):
+    copies = [pltpu.make_async_copy(cor_v, cor_hbm, sem.at[4])]
+    copies[0].start()
+    lhs_g = lhs_v[...]
+    for n in range(4):
+        cols = slice(n * 256, (n + 1) * 256)
+        o = dot3(lhs_g, farh[:, cols], farl[:, cols])
+        re = img_v[0, :, cols] + o[:LH]
+        im = img_v[1, :, cols] + o[LH:]
+        pc = phase[0:1, cols]
+        ps = phase[1:2, cols]
+        buf[0, :, cols] = re * pc - im * ps
+        buf[1, :, cols] = im * pc + re * ps
+        cp = pltpu.make_async_copy(buf.at[:, :, cols], img_hbm.at[:, :, cols], sem.at[n])
         cp.start()
+        copies.append(cp)
     for cp in copies:
         cp.wait()
 
@@ -450,29 +459,31 @@
     vm = pltpu.VMEM
     smem = pl.BlockSpec(memory_space=pltpu.SMEM)
     hbm = pl.BlockSpec(memory_space=pltpu.HBM)
+    vmem = pl.BlockSpec(memory_space=pltpu.VMEM)
     anym = pl.BlockSpec(memory_space=pl.ANY)
     stay = [
         pltpu.with_memory_space_constraint(x, pltpu.HBM)
         for x in (subgrid_start, vis_row, jnp.transpose(vis_weight, (0, 2, 1)), facets)
     ]
-    cor, img = pl.pallas_call(
+    rest = pl.pallas_call(
         kernel,
         out_shape=(
             jax.ShapeDtypeStruct((1, 32, 2, SG), F32),
             jax.ShapeDtypeStruct((2, LH, LW), F32),
+            jax.ShapeDtypeStruct((2 * LH, 256), F32),
+            jax.ShapeDtypeStruct((256, LW), BF16),
+            jax.ShapeDtypeStruct((256, LW), BF16),
+            jax.ShapeDtypeStruct((8, LW), F32),
         ),
         in_specs=[smem, smem, hbm, hbm, hbm, hbm],
-        out_specs=(anym, anym),
+        out_specs=(vmem,) * 6,
         scratch_shapes=[
             pltpu.SMEM((NR,), I32),
             vm((1, MAXB), I32),
             vm((1, 32, MAXB), F32),
             vm((2, LH, LW), F32),
-            vm((2 * LH, LW), BF16),
-            vm((2 * LH, LW), BF16),
-            vm((2, 256, LW), BF16),
-            vm((2, 256, LW), BF16),
-            vm((8, LW), F32),
+            vm((256, LW), BF16),
+            vm((256, LW), BF16),
             vm((2, 2, 2, 2, 2, 32, LH), F32),
             vm((2, 2, 2, 2, 32, LH), F32),
             vm((2, 2, 2, 2, 32, LH), F32),
@@ -489,9 +500,7 @@
             vm((NR, 4, 128), F32),
             vm((NR, 4, 128), F32),
             vm((2, 2, 2, 2, 2, 32, LH), F32),
-            vm((1, 32, 2, SG), F32),
-            vm((2, LH, LW), F32),
-            dma((4,)), dma((5,)), dma((2,)), dma((2,)), dma((2,)), dma((2,)),
+            dma((4,)), dma((2,)), dma((2,)), dma((2,)), dma((2,)),
             dma, dma, dma, dma, dma, dma, dma, dma,
             dma((7,)), dma((7,)), dma((8,)), dma((8,)),
         ],
@@ -503,11 +512,11 @@
             jax.ShapeDtypeStruct((1, 32, 2, SG), F32),
             jax.ShapeDtypeStruct((2, LH, LW), F32),
         ),
-        in_specs=[anym, anym],
+        in_specs=[vmem] * 6,
         out_specs=(hbm, hbm),
-        scratch_shapes=[dma((2,))],
-        compiler_params=pltpu.CompilerParams(vmem_limit_bytes=4 * 1024 * 1024),
-    )(cor, img)
+        scratch_shapes=[vm((2, LH, LW), F32), dma((5,))],
+        compiler_params=pltpu.CompilerParams(vmem_limit_bytes=8 * 1024 * 1024),
+    )(*rest)
 
 
 def solution(mesh):

time: 42.7 us -> 41 us (0.960)
  Pallas kernels: 40.6 us -> 39 us
    pallas_call x1, Pallas kernels: 39.6 us -> 37.5 us  [per_device(): pl.pallas_call(kernel, out_shape=(jax.ShapeDtypeStruct((1, 32, 2, SG), F3...]
    pallas_call x1, Pallas kernels: 1.02 us -> 1.45 us  [per_device(): pl.pallas_call(emit, out_shape=(jax.ShapeDtypeStruct((1, 32, 2, SG), F32)...]
where the time goes in v4:
time: 41 us; the launch traced here: 40.9 us
  Pallas kernels  39 us (95%)
  between operations  1.93 us (5%)
    pallas_call x1, Pallas kernels, per_device(): pl.pallas_call(kernel, out_shape=(jax.ShapeDtypeStruct((1, 32, 2, SG), F3...  37.5 us
    pallas_call x1, Pallas kernels, per_device(): pl.pallas_call(emit, out_shape=(jax.ShapeDtypeStruct((1, 32, 2, SG), F32)...  1.45 us

profile of v4, /device:TPU:1, one launch (start us, length us, event | category | flops | bytes accessed | tf_op | source)
XLA Modules:
  0.0 40.9 jit_solution(15492809027437434612)
XLA Ops:
  1.9 37.5 %shard_map.77 = (f32[1,32,2,512]{3,2,1,0:T(2,128)S(1)}, f32[2,128,1024]{2,1,0:T(8,128)S(1)}, f32[256,256]{1,0:T(8,128)S(1)}, bf16[256,1024]{1,0:T(8,128)(2,1)S(1...) custom-call(s32[1]{0:T(128)S(6)} %copy.8.cs_ref, s32[1]{0:T(128)S(6)} %copy.9.vc_ref, s32[16]{0:T(128)} %ss_hbm.1, ...), custom_call_target="tpu_custom_call" | custom-call | tf_op jit(solution)/shard_map/pallas_call | solution.py:468
  39.5 1.4 %shard_map.78 = (f32[1,32,2,512]{3,2,1,0:T(2,128)}, f32[2,128,1024]{2,1,0:T(8,128)}) custom-call(f32[1,32,2,512]{3,2,1,0:T(2,128)S(1)} %get-tuple-element.8.cor_v, f32[2,128,1024]{2,1,0:T(8,128)S(1)} %get-tuple-element.9.img_v, f32[256,256]{1,0:T(8,128)S(1)} %get-tuple-element.10.lhs_v, bf16[256,1024]{1,0:T(8,128)(2,1)S(1)} %get-tuple-element.11.farh, ...), custom_call_target="tpu_custom_call" | custom-call | tf_op jit(solution)/shard_map/pallas_call | solution.py:509

commit v5 on v4

--- a/solution.py
+++ b/solution.py
@@ -20,6 +20,14 @@
 BF16 = jnp.bfloat16
 I32 = jnp.int32
 MESH = pl.DeviceIdType.MESH
+
+
+def div(a, b):
+    return lax.div(a, jnp.int32(b))
+
+
+def rem(a, b):
+    return lax.rem(a, jnp.int32(b))
 
 
 def iota(shape, axis):
@@ -71,16 +79,19 @@
     snd_b, rec_b, agb,
     load_sem, ks_sem, kr_sem, ys_sem, yr_sem,
     gs_sem, gr_sem, as_sem, ar_sem, cs_sem, cr_sem, bs_sem, br_sem,
-    ags_sem, agr_sem, fws_sem, fwr_sem,
+    ags_sem, agr_sem, fws_sem, fwr_sem, word,
 ):
     r = lax.axis_index("frow")
     c = lax.axis_index("fcol")
-    y = c // 4
-    h = (c // 2) % 2
-    k = c % 2
-    low_y = 1 - y // 2
+    y = div(c, 4)
+    h = rem(div(c, 2), 2)
+    k = rem(c, 2)
+    z = div(r, 2)
+    w_lo = rem(r, 2)
+    low_y = 1 - div(y, 2)
     dev_k = (r, c + 1 - 2 * k)
-    y_of = [y, 3 - y, (y + 2) % 4, (5 - y) % 4]
+    y_of = [y, 3 - y, rem(y + 2, 4), rem(5 - y, 4)]
+    half_of = [1 - div(yy, 2) for yy in y_of]
     h_of = [h, 1 - h]
     near = [(1, 1), (0, 1), (1, 0)]
     far = [(2, 1), (3, 1), (2, 0), (3, 0)]
@@ -92,7 +103,7 @@
     def group(rel):
         return rel[0] // 2
 
-    r_peers = [(r + d) % NR for d in range(NR)]
+    r_peers = [rem(r + d, NR) for d in range(NR)]
     dev_r = [(rp, c) for rp in r_peers]
     by_distance = sorted(range(1, NR), key=lambda d: abs(d - NR // 2))
 
@@ -112,12 +123,14 @@
         cp.start()
 
     barrier = pltpu.get_barrier_semaphore()
-    for dev in [dev_r[d] for d in by_distance] + [dev_yh(rel) for rel in far + near] + [dev_k]:
+    dev_z = [(rem(z + d, 8) * 2 + w_lo, c) for d in (1, 7, 2, 6)]
+    dev_w = (r + 1 - 2 * w_lo, c)
+    for dev in [dev_yh(rel) for rel in far + near] + dev_z[:2] + [dev_w, dev_k]:
         pl.semaphore_signal(barrier, inc=1, device_id=dev, device_id_type=MESH)
 
     f = cs_ref[0]
     off = c * LW
-    pair = (y + 1) // 2 % 2
+    pair = rem(div(y + 1, 2), 2)
     base_of = [128 * (1 - pair), 128 * pair]
     u = iota((16, 128), 0)
     place = off + iota((16, 128), 1)
@@ -186,31 +199,34 @@
                 part[g, 1 - kk, 1, 1 - hh, 1] = ai + br
 
     strip_group(1)
-    pl.semaphore_wait(barrier, 23)
-    k_copies = [
-        remote(part.at[g, 1 - k], rec_k.at[g], ks_sem.at[g], kr_sem.at[g], dev_k) for g in range(2)
-    ]
-    k_copies[1].start()
+    pl.semaphore_wait(barrier, 11)
+    for dev in dev_z[:2]:
+        pl.semaphore_signal(word.at[0], inc=1, device_id=dev, device_id_type=MESH)
+    order = far + near + [(0, 0)]
+
+    def cell(rel):
+        return group(rel), half_of[rel[0]], h_of[rel[1]]
+
+    def k_copy(i):
+        g, sg, hh = cell(order[i])
+        return remote(part.at[g, 1 - k, sg, hh], rec_k.at[g, sg, hh], ks_sem, kr_sem.at[i], dev_k)
+
+    for i in range(4):
+        k_copy(i).start()
     strip_group(0)
-    k_copies[0].start()
-
-    def send_group(g, group_rels):
-        k_copies[g].wait_recv()
-        for sg in range(2):
-            for hh in range(2):
-                snd_y[g, sg, hh] = part[g, k, sg, hh] + rec_k[g, sg, hh]
-        copies = [
+    for i in range(4, 8):
+        k_copy(i).start()
+    for i, rel in enumerate(order):
+        g, sg, hh = cell(rel)
+        k_copy(i).wait_recv()
+        snd_y[g, sg, hh] = part[g, k, sg, hh] + rec_k[g, sg, hh]
+        if i < 7:
             remote(
-                snd_y.at[g, 1 - y_of[rel[0]] // 2, h_of[rel[1]]],
-                rec_y.at[rels.index(rel)], ys_sem.at[g], yr_sem.at[g], dev_yh(rel),
-            )
-            for rel in group_rels
-        ]
-        for cp in copies:
-            cp.start()
-
-    send_group(1, far)
-    send_group(0, near)
+                snd_y.at[g, sg, hh], rec_y.at[rels.index(rel)], ys_sem, yr_sem.at[g], dev_yh(rel)
+            ).start()
+    pl.semaphore_wait(word.at[0], 2)
+    for dev in dev_z[2:]:
+        pl.semaphore_signal(word.at[1], inc=1, device_id=dev, device_id_type=MESH)
 
     for cp in small:
         cp.wait()
@@ -252,6 +268,9 @@
     farh[...] = tables[1][0]
     farl[...] = tables[1][1]
 
+    pl.semaphore_wait(word.at[1], 2)
+    pl.semaphore_signal(word.at[2], inc=1, device_id=dev_w, device_id_type=MESH)
+
     mu = iota((16, 128), 0)
     lb = iota((16, 128), 1)
 
@@ -271,6 +290,7 @@
             v = jnp.where(blk < 2, hi, jnp.where(blk == 2, v - hi, 0.0))
             d1[po, rows, :] = v.astype(BF16)
 
+    pl.semaphore_wait(word.at[2], 1)
     exchange(gai_s, gai_r, r, gs_sem, gr_sem)
     gai_r[r] = gai_s[r]
 
@@ -301,8 +321,8 @@
 
     far_in = rec_y.at[pl.ds(3, 4)]
     near_in = rec_y.at[pl.ds(0, 3)]
-    far_all = remote(far_in, far_in, ys_sem.at[1], yr_sem.at[1], dev_yh(far[0]))
-    near_all = remote(near_in, near_in, ys_sem.at[0], yr_sem.at[0], dev_yh(near[0]))
+    far_all = remote(far_in, far_in, ys_sem, yr_sem.at[1], dev_yh(far[0]))
+    near_all = remote(near_in, near_in, ys_sem, yr_sem.at[0], dev_yh(near[0]))
     near_all.wait_recv()
     far_all.wait_recv()
     strip = (
@@ -330,10 +350,13 @@
         re = zre[:, q * 128 : (q + 1) * 128]
         im = zim[:, q * 128 : (q + 1) * 128]
         cols += [re * tc + im * ts, im * tc - re * ts]
-    sub = dot3(jnp.concatenate(cols, axis=1), e3h, e3l)
+    zh, zl = split(jnp.concatenate(cols, axis=1))
+    wide_s = dot(zh, jnp.concatenate([e3h, e3l], axis=1))
+    sub = wide_s[:, :128] + (wide_s[:, 128:] + dot(zl, e3h))
     grid = sub * gai_r[...].reshape(256, 128)
     g_s[...] = grid.reshape(NR, 16, 128)
-    vv = dot3(grid, e4h, e4l)
+    gh, gl = split(grid)
+    vv = dot(jnp.concatenate([gh, gl], axis=1), jnp.concatenate([e4h, e4h], axis=0)) + dot(gh, e4l)
     res = []
     ims = []
     for q in range(2):
@@ -359,29 +382,29 @@
 
     mine = agb.at[0, k, low_y, h]
     sends = [
-        remote(mine, agb.at[group(rel), k, low_y, h], ags_sem.at[i], agr_sem.at[i], dev_yh(rel))
+        remote(mine, agb.at[group(rel), k, low_y, h], ags_sem, agr_sem.at[i], dev_yh(rel))
         for i, rel in enumerate(rels)
     ]
     for cp in sends[3:] + sends[:3]:
         cp.start()
 
     def block(rel, kk):
-        return agb.at[group(rel), kk, 1 - y_of[rel[0]] // 2, h_of[rel[1]]]
+        return agb.at[group(rel), kk, half_of[rel[0]], h_of[rel[1]]]
 
     forwards = [
-        remote(block(rel, k), block(rel, k), fws_sem.at[i], fwr_sem.at[i], dev_k)
+        remote(block(rel, k), block(rel, k), fws_sem, fwr_sem.at[i], dev_k)
         for i, rel in enumerate(rels + [(0, 0)])
     ]
     forwards[7].start()
 
     def arrive(i):
         ref = block(rels[i], k)
-        remote(ref, ref, ags_sem.at[i], agr_sem.at[i], dev_yh(rels[i])).wait_recv()
+        remote(ref, ref, ags_sem, agr_sem.at[i], dev_yh(rels[i])).wait_recv()
         forwards[i].start()
 
     def forwarded(i):
         ref = block((rels + [(0, 0)])[i], 1 - k)
-        remote(ref, ref, fws_sem.at[i], fwr_sem.at[i], dev_k).wait_recv()
+        remote(ref, ref, fws_sem, fwr_sem.at[i], dev_k).wait_recv()
 
     all_of(g_r, cs_sem, cr_sem).wait_recv()
     lane = iota((256, SG), 1)
@@ -424,10 +447,10 @@
         forwarded(i)
     lhs_v[...] = image_lhs(1)
 
-    for cp in k_copies + sends + forwards:
-        cp.wait_send()
-    far_all.wait_send()
-    near_all.wait_send()
+    remote(rec_k, rec_k, ks_sem, kr_sem.at[0], dev_k).wait_send()
+    remote(rec_k, rec_k, fws_sem, fwr_sem.at[0], dev_k).wait_send()
+    remote(rec_y, rec_y, ys_sem, yr_sem.at[0], dev_k).wait_send()
+    remote(rec_y, rec_y, ags_sem, agr_sem.at[0], dev_k).wait_send()
     all_of(gai_r, gs_sem, gr_sem).wait_send()
     all_of(rec_a, as_sem, ar_sem).wait_send()
     all_of(g_r, cs_sem, cr_sem).wait_send()
@@ -500,9 +523,9 @@
             vm((NR, 4, 128), F32),
             vm((NR, 4, 128), F32),
             vm((2, 2, 2, 2, 2, 32, LH), F32),
-            dma((4,)), dma((2,)), dma((2,)), dma((2,)), dma((2,)),
+            dma((4,)), dma, dma((8,)), dma, dma((2,)),
             dma, dma, dma, dma, dma, dma, dma, dma,
-            dma((7,)), dma((7,)), dma((8,)), dma((8,)),
+            dma, dma((7,)), dma, dma((8,)), pltpu.SemaphoreType.REGULAR((3,)),
         ],
         compiler_params=pltpu.CompilerParams(collective_id=0, has_side_effects=True, vmem_limit_bytes=16 * 1024 * 1024),
     )(column_start, vis_count, *stay)

time: 41 us -> 39.8 us (0.971)
  Pallas kernels: 39 us -> 37.8 us
    pallas_call x1, Pallas kernels: 37.5 us -> 36.3 us  [per_device(): pl.pallas_call(kernel, out_shape=(jax.ShapeDtypeStruct((1, 32, 2, SG), F3...]
where the time goes in v5:
time: 39.8 us; the launch traced here: 39.7 us
  Pallas kernels  37.8 us (95%)
  between operations  1.93 us (5%)
    pallas_call x1, Pallas kernels, per_device(): pl.pallas_call(kernel, out_shape=(jax.ShapeDtypeStruct((1, 32, 2, SG), F3...  36.3 us
    pallas_call x1, Pallas kernels, per_device(): pl.pallas_call(emit, out_shape=(jax.ShapeDtypeStruct((1, 32, 2, SG), F32)...  1.45 us

profile of v5, /device:TPU:1, one launch (start us, length us, event | category | flops | bytes accessed | tf_op | source)
XLA Modules:
  0.0 39.7 jit_solution(410657025918504560)
XLA Ops:
  1.9 36.3 %shard_map.77 = (f32[1,32,2,512]{3,2,1,0:T(2,128)S(1)}, f32[2,128,1024]{2,1,0:T(8,128)S(1)}, f32[256,256]{1,0:T(8,128)S(1)}, bf16[256,1024]{1,0:T(8,128)(2,1)S(1...) custom-call(s32[1]{0:T(128)S(6)} %copy.8.cs_ref, s32[1]{0:T(128)S(6)} %copy.9.vc_ref, s32[16]{0:T(128)} %ss_hbm.1, ...), custom_call_target="tpu_custom_call" | custom-call | tf_op jit(solution)/shard_map/pallas_call | solution.py:491
  38.2 1.4 %shard_map.78 = (f32[1,32,2,512]{3,2,1,0:T(2,128)}, f32[2,128,1024]{2,1,0:T(8,128)}) custom-call(f32[1,32,2,512]{3,2,1,0:T(2,128)S(1)} %get-tuple-element.8.cor_v, f32[2,128,1024]{2,1,0:T(8,128)S(1)} %get-tuple-element.9.img_v, f32[256,256]{1,0:T(8,128)S(1)} %get-tuple-element.10.lhs_v, bf16[256,1024]{1,0:T(8,128)(2,1)S(1)} %get-tuple-element.11.farh, ...), custom_call_target="tpu_custom_call" | custom-call | tf_op jit(solution)/shard_map/pallas_call | solution.py:532

commit v6 on v5

--- a/solution.py
+++ b/solution.py
@@ -385,8 +385,8 @@
         remote(mine, agb.at[group(rel), k, low_y, h], ags_sem, agr_sem.at[i], dev_yh(rel))
         for i, rel in enumerate(rels)
     ]
-    for cp in sends[3:] + sends[:3]:
-        cp.start()
+    for i in (3, 4, 0, 5, 1, 6, 2):
+        sends[i].start()
 
     def block(rel, kk):
         return agb.at[group(rel), kk, half_of[rel[0]], h_of[rel[1]]]
@@ -417,7 +417,7 @@
             ex = ((rowi & 127) == (q * 2 + p) * 32 + (lane >> 4)).astype(F32).astype(BF16)
             wide_g = jnp.where(keep, dot(gath, ex), 0.0)
             cor_v[0, pl.ds(qq * 16, 16), p, :] = jnp.sum(wide_g.reshape(16, 16, SG), axis=1)
-    for i in range(7):
+    for i in (2, 6, 5, 1, 0, 4, 3):
         arrive(i)
 
     def image_lhs(g):

time: 39.8 us -> 39.7 us (level)
  no operation moved by 1% of the time
where the time goes in v6:
time: 39.7 us; the launch traced here: 39.6 us
  Pallas kernels  37.7 us (95%)
  between operations  1.93 us (5%)
    pallas_call x1, Pallas kernels, per_device(): pl.pallas_call(kernel, out_shape=(jax.ShapeDtypeStruct((1, 32, 2, SG), F3...  36.2 us
    pallas_call x1, Pallas kernels, per_device(): pl.pallas_call(emit, out_shape=(jax.ShapeDtypeStruct((1, 32, 2, SG), F32)...  1.45 us

profile of v6, /device:TPU:1, one launch (start us, length us, event | category | flops | bytes accessed | tf_op | source)
XLA Modules:
  0.0 39.6 jit_solution(17980107291342706893)
XLA Ops:
  1.9 36.2 %shard_map.77 = (f32[1,32,2,512]{3,2,1,0:T(2,128)S(1)}, f32[2,128,1024]{2,1,0:T(8,128)S(1)}, f32[256,256]{1,0:T(8,128)S(1)}, bf16[256,1024]{1,0:T(8,128)(2,1)S(1...) custom-call(s32[1]{0:T(128)S(6)} %copy.8.cs_ref, s32[1]{0:T(128)S(6)} %copy.9.vc_ref, s32[16]{0:T(128)} %ss_hbm.1, ...), custom_call_target="tpu_custom_call" | custom-call | tf_op jit(solution)/shard_map/pallas_call | solution.py:491
  38.1 1.4 %shard_map.78 = (f32[1,32,2,512]{3,2,1,0:T(2,128)}, f32[2,128,1024]{2,1,0:T(8,128)}) custom-call(f32[1,32,2,512]{3,2,1,0:T(2,128)S(1)} %get-tuple-element.8.cor_v, f32[2,128,1024]{2,1,0:T(8,128)S(1)} %get-tuple-element.9.img_v, f32[256,256]{1,0:T(8,128)S(1)} %get-tuple-element.10.lhs_v, bf16[256,1024]{1,0:T(8,128)(2,1)S(1)} %get-tuple-element.11.farh, ...), custom_call_target="tpu_custom_call" | custom-call | tf_op jit(solution)/shard_map/pallas_call | solution.py:532

commit v7 on v5

--- a/solution.py
+++ b/solution.py
@@ -152,17 +152,18 @@
 
     columns = [[], []]
     waves = []
+    nears = []
     for n in range(8):
-        for g in range(2):
-            columns[g].append(table_tile(g, now[0], now[1]))
+        columns[1].append(table_tile(1, now[0], now[1]))
+        nears.append((now[0], now[1]))
         waves.append([w[0:1] * F32(1.0 / math.sqrt(N2)) for w in now[2]])
         now = [
             (ca * cb - sa * sb, sa * cb + ca * sb) for (ca, sa), (cb, sb) in zip(now, step)
         ]
-    tables = [
-        [jnp.concatenate([t[e] for t in columns[g]], axis=1) for e in range(2)] for g in range(2)
-    ]
-
+    for near_ab in nears:
+        columns[0].append(table_tile(0, *near_ab))
+    tabh[...] = jnp.concatenate([t[0] for t in columns[0]], axis=1)
+    tabl[...] = jnp.concatenate([t[1] for t in columns[0]], axis=1)
     load.wait()
     parts = []
     for n in range(8):
@@ -182,8 +183,11 @@
         )
     rhi, rlo = [jnp.concatenate([t[e] for t in parts], axis=1) for e in range(2)]
 
-    def strip_group(g):
-        th, tl = tables[g]
+    tables = [
+        [jnp.concatenate([t[e] for t in columns[g]], axis=1) for e in range(2)] for g in range(2)
+    ]
+
+    def strip_group(g, th, tl):
         both = dot_t(jnp.concatenate([th, tl], axis=0), rhi)
         acc = both[:256] + (dot_t(th, rlo) + both[256:])
         for hh in range(2):
@@ -198,7 +202,7 @@
                 part[g, 1 - kk, 1, 1 - hh, 0] = ar - bi
                 part[g, 1 - kk, 1, 1 - hh, 1] = ai + br
 
-    strip_group(1)
+    strip_group(1, *tables[1])
     pl.semaphore_wait(barrier, 11)
     for dev in dev_z[:2]:
         pl.semaphore_signal(word.at[0], inc=1, device_id=dev, device_id_type=MESH)
@@ -213,7 +217,7 @@
 
     for i in range(4):
         k_copy(i).start()
-    strip_group(0)
+    strip_group(0, tabh[...], tabl[...])
     for i in range(4, 8):
         k_copy(i).start()
     for i, rel in enumerate(order):
@@ -263,8 +267,6 @@
         some = dst.at[pl.ds(0, NR - 1)]
         return remote(some, some, ssem, rsem, dev_r[1])
 
-    tabh[...] = tables[0][0]
-    tabl[...] = tables[0][1]
     farh[...] = tables[1][0]
     farl[...] = tables[1][1]
 

time: 39.8 us -> 40 us (level)
  no operation moved by 1% of the time
where the time goes in v7:
time: 40 us; the launch traced here: 39.9 us
  Pallas kernels  37.9 us (95%)
  between operations  1.93 us (5%)
    pallas_call x1, Pallas kernels, per_device(): pl.pallas_call(kernel, out_shape=(jax.ShapeDtypeStruct((1, 32, 2, SG), F3...  36.5 us
    pallas_call x1, Pallas kernels, per_device(): pl.pallas_call(emit, out_shape=(jax.ShapeDtypeStruct((1, 32, 2, SG), F32)...  1.45 us

profile of v7, /device:TPU:1, one launch (start us, length us, event | category | flops | bytes accessed | tf_op | source)
XLA Modules:
  0.0 39.9 jit_solution(3970556859894067761)
XLA Ops:
  1.9 36.5 %shard_map.77 = (f32[1,32,2,512]{3,2,1,0:T(2,128)S(1)}, f32[2,128,1024]{2,1,0:T(8,128)S(1)}, f32[256,256]{1,0:T(8,128)S(1)}, bf16[256,1024]{1,0:T(8,128)(2,1)S(1...) custom-call(s32[1]{0:T(128)S(6)} %copy.8.cs_ref, s32[1]{0:T(128)S(6)} %copy.9.vc_ref, s32[16]{0:T(128)} %ss_hbm.1, ...), custom_call_target="tpu_custom_call" | custom-call | tf_op jit(solution)/shard_map/pallas_call | solution.py:493
  38.4 1.4 %shard_map.78 = (f32[1,32,2,512]{3,2,1,0:T(2,128)}, f32[2,128,1024]{2,1,0:T(8,128)}) custom-call(f32[1,32,2,512]{3,2,1,0:T(2,128)S(1)} %get-tuple-element.8.cor_v, f32[2,128,1024]{2,1,0:T(8,128)S(1)} %get-tuple-element.9.img_v, f32[256,256]{1,0:T(8,128)S(1)} %get-tuple-element.10.lhs_v, bf16[256,1024]{1,0:T(8,128)(2,1)S(1)} %get-tuple-element.11.farh, ...), custom_call_target="tpu_custom_call" | custom-call | tf_op jit(solution)/shard_map/pallas_call | solution.py:534

commit v8 on v7

--- a/solution.py
+++ b/solution.py
@@ -125,7 +125,8 @@
     barrier = pltpu.get_barrier_semaphore()
     dev_z = [(rem(z + d, 8) * 2 + w_lo, c) for d in (1, 7, 2, 6)]
     dev_w = (r + 1 - 2 * w_lo, c)
-    for dev in [dev_yh(rel) for rel in far + near] + dev_z[:2] + [dev_w, dev_k]:
+    by_hops = [(3, 1), (1, 1), (0, 1), (3, 0), (1, 0)]
+    for dev in [dev_yh(rel) for rel in by_hops] + dev_z[:2] + [dev_w, dev_k]:
         pl.semaphore_signal(barrier, inc=1, device_id=dev, device_id_type=MESH)
 
     f = cs_ref[0]
@@ -203,7 +204,10 @@
                 part[g, 1 - kk, 1, 1 - hh, 1] = ai + br
 
     strip_group(1, *tables[1])
-    pl.semaphore_wait(barrier, 11)
+    pl.semaphore_wait(barrier, 9)
+    pl.semaphore_signal(
+        word.at[3], inc=1, device_id=(r, rem(y + 3, 4) * 4 + h * 2 + k), device_id_type=MESH
+    )
     for dev in dev_z[:2]:
         pl.semaphore_signal(word.at[0], inc=1, device_id=dev, device_id_type=MESH)
     order = far + near + [(0, 0)]
@@ -220,6 +224,7 @@
     strip_group(0, tabh[...], tabl[...])
     for i in range(4, 8):
         k_copy(i).start()
+    pl.semaphore_wait(word.at[3], 1)
     for i, rel in enumerate(order):
         g, sg, hh = cell(rel)
         k_copy(i).wait_recv()
@@ -527,7 +532,7 @@
             vm((2, 2, 2, 2, 2, 32, LH), F32),
             dma((4,)), dma, dma((8,)), dma, dma((2,)),
             dma, dma, dma, dma, dma, dma, dma, dma,
-            dma, dma((7,)), dma, dma((8,)), pltpu.SemaphoreType.REGULAR((3,)),
+            dma, dma((7,)), dma, dma((8,)), pltpu.SemaphoreType.REGULAR((4,)),
         ],
         compiler_params=pltpu.CompilerParams(collective_id=0, has_side_effects=True, vmem_limit_bytes=16 * 1024 * 1024),
     )(column_start, vis_count, *stay)

time: 40 us -> 40 us (level)
  no operation moved by 1% of the time
where the time goes in v8:
time: 40 us; the launch traced here: 39.8 us
  Pallas kernels  37.9 us (95%)
  between operations  1.93 us (5%)
    pallas_call x1, Pallas kernels, per_device(): pl.pallas_call(kernel, out_shape=(jax.ShapeDtypeStruct((1, 32, 2, SG), F3...  36.5 us
    pallas_call x1, Pallas kernels, per_device(): pl.pallas_call(emit, out_shape=(jax.ShapeDtypeStruct((1, 32, 2, SG), F32)...  1.45 us

profile of v8, /device:TPU:1, one launch (start us, length us, event | category | flops | bytes accessed | tf_op | source)
XLA Modules:
  0.0 39.8 jit_solution(4159682906949106086)
XLA Ops:
  1.9 36.5 %shard_map.77 = (f32[1,32,2,512]{3,2,1,0:T(2,128)S(1)}, f32[2,128,1024]{2,1,0:T(8,128)S(1)}, f32[256,256]{1,0:T(8,128)S(1)}, bf16[256,1024]{1,0:T(8,128)(2,1)S(1...) custom-call(s32[1]{0:T(128)S(6)} %copy.8.cs_ref, s32[1]{0:T(128)S(6)} %copy.9.vc_ref, s32[16]{0:T(128)} %ss_hbm.1, ...), custom_call_target="tpu_custom_call" | custom-call | tf_op jit(solution)/shard_map/pallas_call | solution.py:498
  38.4 1.4 %shard_map.78 = (f32[1,32,2,512]{3,2,1,0:T(2,128)}, f32[2,128,1024]{2,1,0:T(8,128)}) custom-call(f32[1,32,2,512]{3,2,1,0:T(2,128)S(1)} %get-tuple-element.8.cor_v, f32[2,128,1024]{2,1,0:T(8,128)S(1)} %get-tuple-element.9.img_v, f32[256,256]{1,0:T(8,128)S(1)} %get-tuple-element.10.lhs_v, bf16[256,1024]{1,0:T(8,128)(2,1)S(1)} %get-tuple-element.11.farh, ...), custom_call_target="tpu_custom_call" | custom-call | tf_op jit(solution)/shard_map/pallas_call | solution.py:539
